TPU v7x, 32 devices: a whole 2x2x4 slice. The times are simulated.
32 devices in a mesh: dp: 2 (over x), ctx: 4 (over y, core), tp: 4 (over z).
Axes of the slice: x: 2, y: 2, z: 4, core: 2. Of those that a mesh axis runs over, the one named last changes fastest.
Arguments:
- tokens: bfloat16 [16384, 768], P(('dp', 'ctx', 'tp')), may hold values from -6 to 6
- first_gain: bfloat16 [768], replicated, may hold values from 0.5 to 1.5
- first_bias: bfloat16 [768], replicated, may hold values from -0.4375 to 0.4375
- mixer_weight: bfloat16 [768, 3, 768], P(None, None, 'tp'), may hold values from -0.21875 to 0.21875
- mixer_bias: bfloat16 [3, 768], P(None, 'tp'), may hold values from -0.3125 to 0.3125
- feature_weight: bfloat16 [2, 12, 64, 64], P(None, 'tp'), may hold values from -1.5 to 1.5
- feature_bias: bfloat16 [2, 12, 64], P(None, 'tp'), may hold values from -6 to 6
- output_weight: bfloat16 [768, 768], P('tp'), may hold values from -6 to 6
- output_bias: bfloat16 [768], replicated, may hold values from -4 to 4
- second_gain: bfloat16 [768], replicated, may hold values from 0.5 to 1.5
- second_bias: bfloat16 [768], replicated, may hold values from -4 to 4
- inner_weight: bfloat16 [768, 3072], P(None, 'tp'), may hold values from -0.21875 to 0.21875
- inner_bias: bfloat16 [3072], P('tp'), may hold values from -4 to 4
- outer_weight: bfloat16 [3072, 768], P('tp'), may hold values from -0.109375 to 0.109375
- outer_bias: bfloat16 [768], replicated, may hold values from -4 to 4
- block_owner: int32 [2, 32], P('dp'), may hold values from 0 to 0, as said below
- cotangent: bfloat16 [16384, 768], P(('dp', 'ctx', 'tp')), may hold values from -6 to 6
Outputs:
- result: bfloat16 [16384, 768], P(('dp', 'ctx', 'tp'))
- tokens_gradient: float32 [16384, 768], P(('dp', 'ctx', 'tp'))
- first_gain_gradient: float32 [768], replicated
- first_bias_gradient: float32 [768], replicated
- mixer_weight_gradient: float32 [768, 3, 768], P(None, None, 'tp')
- mixer_bias_gradient: float32 [3, 768], P(None, 'tp')
- feature_weight_gradient: float32 [2, 12, 64, 64], P(None, 'tp')
- feature_bias_gradient: float32 [2, 12, 64], P(None, 'tp')
- output_weight_gradient: float32 [768, 768], P('tp')
- output_bias_gradient: float32 [768], replicated
- second_gain_gradient: float32 [768], replicated
- second_bias_gradient: float32 [768], replicated
- inner_weight_gradient: float32 [768, 3072], P(None, 'tp')
- inner_bias_gradient: float32 [3072], P('tp')
- outer_weight_gradient: float32 [3072, 768], P('tp')
- outer_bias_gradient: float32 [768], replicated
Inputs may be any that keep to these rules, and one draw needn't show every extreme that they name: `block_owner`: all blocks of one sequence carry one number, and pieces of a data group share the same blocks. A sequence covers 8192 // 256 or twice that many consecutive blocks of every piece, so it has 8192 or 16384 tokens; its number is the index of its last 8192-token unit, so numbers rise along a row, differ between sequences, and the last block of every row carries 1 - 1.
All inputs are finite; a program needn't handle non-finite values.
Results may differ from a plain program's by a relative error of at most 0.015.
Values may be sent and summed in bfloat16 or wider, within the bound.
A program may use at most 128 MiB of HBM per device.

v0:
```python
import jax
import jax.numpy as jnp
from jax import lax
from jax.sharding import PartitionSpec as P

HD = 64
BLOCK = 64
SHORT = 8192


EPSILON = 1e-05
HIGHEST = lax.Precision.HIGHEST


def entering(x, axis, combine, identity, reverse):
    peers, mine = (lax.axis_size(axis), lax.axis_index(axis))
    everything = jax.tree.map(lambda part: lax.all_gather(part, axis), x)
    start = jax.tree.map(
        lambda part, zero: jnp.broadcast_to(jnp.asarray(zero, part.dtype), part.shape), x, identity
    )

    def turn(k, before):
        at = peers - 1 - k if reverse else k
        reached = at > mine if reverse else at < mine
        new = combine(before, jax.tree.map(lambda part: part[at], everything))
        return jax.tree.map(lambda a, b: jnp.where(reached, a, b), new, before)

    return lax.fori_loop(0, peers, turn, start)


def layer_norm(values, norm_gain, norm_offset):
    average = jnp.mean(values, axis=-1, keepdims=True)
    centered = values - average
    variance = jnp.mean(centered * centered, axis=-1, keepdims=True)
    return centered * lax.rsqrt(variance + EPSILON) * norm_gain + norm_offset


def gaussian_unit(values):
    return (
        0.5
        * values
        * (1.0 + jnp.tanh(0.7978845608028654 * (values + 0.044715 * values * values * values)))
    )


def feature_map(inputs, weight, offset):
    logits = jnp.einsum("thd,hde->the", inputs, weight, precision=HIGHEST) + offset
    return jnp.concatenate(
        [jax.nn.softmax(logits, axis=-1), jax.nn.softmax(-logits, axis=-1)], axis=-1
    )


def rounded(values):
    return lax.optimization_barrier(values.astype(jnp.bfloat16)).astype(jnp.float32)


def add_pair(first_pair, second_pair):
    return (first_pair[0] + second_pair[0], first_pair[1] + second_pair[1])


def shards(
    tokens,
    first_gain,
    first_bias,
    mixer_weight,
    mixer_bias,
    feature_weight,
    feature_bias,
    output_weight,
    output_bias,
    second_gain,
    second_bias,
    inner_weight,
    inner_bias,
    outer_weight,
    outer_bias,
    block_owner,
    cotangent,
):
    local_rows, model_width = tokens.shape
    heads_here = mixer_weight.shape[2] // HD
    piece_rows = local_rows * lax.axis_size("tp")
    blocks = piece_rows // BLOCK
    unit_count = piece_rows * lax.axis_size("ctx") // SHORT
    owners = block_owner[0]
    block_index = jnp.arange(blocks)
    member = (owners[:, None] == jnp.arange(unit_count)[None, :]).astype(jnp.float32)
    earlier = (
        (owners[:, None] == owners[None, :]) & (block_index[:, None] > block_index[None, :])
    ).astype(jnp.float32)
    causal = jnp.arange(BLOCK)[:, None] >= jnp.arange(BLOCK)[None, :]
    inputs = tokens.astype(jnp.float32)
    first_normed, first_pull = jax.vjp(
        layer_norm, inputs, first_gain.astype(jnp.float32), first_bias.astype(jnp.float32)
    )
    first_low = first_normed.astype(jnp.bfloat16)
    first_rows = lax.all_gather(first_low, "tp", axis=0, tiled=True)
    mixer_flat = mixer_weight.reshape(model_width, -1)
    mixed_rows = jnp.dot(
        first_rows, mixer_flat, preferred_element_type=jnp.float32
    ) + mixer_bias.astype(jnp.float32).reshape(-1)
    mixed_low = mixed_rows.astype(jnp.bfloat16).reshape(piece_rows, 3, heads_here, HD)
    query_rows = mixed_low[:, 0]
    key_rows = mixed_low[:, 1]
    value_rows = mixed_low[:, 2]
    weight_float = feature_weight.astype(jnp.float32)
    bias_float = feature_bias.astype(jnp.float32)
    query_lifted, query_pull = jax.vjp(
        feature_map, query_rows.astype(jnp.float32), weight_float[0], bias_float[0]
    )
    key_lifted, key_pull = jax.vjp(
        feature_map, key_rows.astype(jnp.float32), weight_float[1], bias_float[1]
    )
    query_blocks = query_lifted.astype(jnp.bfloat16).reshape(blocks, BLOCK, heads_here, 2 * HD)
    key_blocks = key_lifted.astype(jnp.bfloat16).reshape(blocks, BLOCK, heads_here, 2 * HD)
    value_blocks = value_rows.reshape(blocks, BLOCK, heads_here, HD)
    block_state = jnp.einsum(
        "jthe,jthf->jhef", value_blocks, key_blocks, preferred_element_type=jnp.float32
    )
    block_norm = jnp.sum(key_blocks.astype(jnp.float32), axis=1)
    totals = (
        jnp.einsum("js,jhef->shef", member, block_state, precision=HIGHEST),
        jnp.einsum("js,jhf->shf", member, block_norm, precision=HIGHEST),
    )
    incoming = entering(
        (totals[0], totals[1]),
        "ctx",
        add_pair,
        (jnp.zeros_like(totals[0]), jnp.zeros_like(totals[1])),
        False,
    )
    state_before = jnp.einsum(
        "ji,ihef->jhef", earlier, block_state, precision=HIGHEST
    ) + jnp.einsum("js,shef->jhef", member, incoming[0], precision=HIGHEST)
    norm_before = jnp.einsum("ji,ihf->jhf", earlier, block_norm, precision=HIGHEST) + jnp.einsum(
        "js,shf->jhf", member, incoming[1], precision=HIGHEST
    )
    numerator = jnp.einsum(
        "jthf,jhef->jthe",
        query_blocks,
        state_before,
        precision=HIGHEST,
        preferred_element_type=jnp.float32,
    )
    denominator = jnp.einsum(
        "jthf,jhf->jth",
        query_blocks,
        norm_before,
        precision=HIGHEST,
        preferred_element_type=jnp.float32,
    )
    scores = jnp.einsum(
        "jthf,jshf->jhts", query_blocks, key_blocks, preferred_element_type=jnp.float32
    )
    scores_low = jnp.where(causal, scores, 0.0).astype(jnp.bfloat16)
    numerator = numerator + jnp.einsum(
        "jhts,jshe->jthe", scores_low, value_blocks, preferred_element_type=jnp.float32
    )
    denominator = denominator + jnp.swapaxes(jnp.sum(scores_low.astype(jnp.float32), axis=-1), 1, 2)
    attended = numerator / denominator[..., None]
    attended_low = attended.astype(jnp.bfloat16).reshape(piece_rows, heads_here * HD)
    attention_sum = lax.psum_scatter(
        jnp.dot(attended_low, output_weight, preferred_element_type=jnp.float32),
        "tp",
        scatter_dimension=0,
        tiled=True,
    )
    middle = inputs + attention_sum + output_bias.astype(jnp.float32)
    second_normed, second_pull = jax.vjp(
        layer_norm, middle, second_gain.astype(jnp.float32), second_bias.astype(jnp.float32)
    )
    second_low = second_normed.astype(jnp.bfloat16)
    second_rows = lax.all_gather(second_low, "tp", axis=0, tiled=True)
    hidden_input = jnp.dot(
        second_rows, inner_weight, preferred_element_type=jnp.float32
    ) + inner_bias.astype(jnp.float32)
    activated_float, curve_pull = jax.vjp(gaussian_unit, hidden_input)
    activated = activated_float.astype(jnp.bfloat16)
    branch_out = lax.psum_scatter(
        jnp.dot(activated, outer_weight, preferred_element_type=jnp.float32).astype(jnp.bfloat16),
        "tp",
        scatter_dimension=0,
        tiled=True,
    ).astype(jnp.float32)
    result = (middle + branch_out + outer_bias.astype(jnp.float32)).astype(jnp.bfloat16)
    upstream = cotangent.astype(jnp.float32)
    upstream_rows = lax.all_gather(cotangent, "tp", axis=0, tiled=True)
    outer_delta = jnp.einsum(
        "tf,td->fd", activated, upstream_rows, preferred_element_type=jnp.float32
    )
    activated_delta = jnp.einsum(
        "td,fd->tf", upstream_rows, outer_weight, preferred_element_type=jnp.float32
    )
    (hidden_delta,) = curve_pull(activated_delta)
    hidden_low = hidden_delta.astype(jnp.bfloat16)
    inner_bias_delta = jnp.sum(hidden_low.astype(jnp.float32), axis=0)
    inner_delta = jnp.einsum(
        "td,tf->df", second_rows, hidden_low, preferred_element_type=jnp.float32
    )
    second_delta = lax.psum_scatter(
        jnp.einsum("tf,df->td", hidden_low, inner_weight, preferred_element_type=jnp.float32),
        "tp",
        scatter_dimension=0,
        tiled=True,
    )
    middle_back, second_gain_part, second_bias_part = second_pull(second_delta)
    middle_delta = upstream + middle_back
    middle_low = middle_delta.astype(jnp.bfloat16)
    middle_rows = lax.all_gather(middle_low, "tp", axis=0, tiled=True)
    output_delta = jnp.einsum(
        "tk,td->kd", attended_low, middle_rows, preferred_element_type=jnp.float32
    )
    attended_delta = rounded(
        jnp.einsum("td,kd->tk", middle_rows, output_weight, preferred_element_type=jnp.float32)
    )
    attended_delta = attended_delta.reshape(blocks, BLOCK, heads_here, HD)
    numerator_delta = attended_delta / denominator[..., None]
    denominator_delta = -jnp.sum(attended_delta * attended, axis=-1) / denominator
    score_delta = (
        jnp.einsum(
            "jthe,jshe->jhts",
            numerator_delta,
            value_blocks,
            precision=HIGHEST,
            preferred_element_type=jnp.float32,
        )
        + jnp.swapaxes(denominator_delta, 1, 2)[..., None]
    )
    score_low = jnp.where(causal, score_delta, 0.0).astype(jnp.bfloat16)
    value_delta = jnp.einsum(
        "jhts,jthe->jshe",
        scores_low,
        numerator_delta,
        precision=HIGHEST,
        preferred_element_type=jnp.float32,
    )
    query_delta = (
        jnp.einsum("jhts,jshf->jthf", score_low, key_blocks, preferred_element_type=jnp.float32)
        + jnp.einsum(
            "jthe,jhef->jthf",
            numerator_delta,
            state_before,
            precision=HIGHEST,
            preferred_element_type=jnp.float32,
        )
        + denominator_delta[..., None] * norm_before[:, None]
    )
    key_delta = jnp.einsum(
        "jhts,jthf->jshf", score_low, query_blocks, preferred_element_type=jnp.float32
    )
    before_delta = jnp.einsum(
        "jthf,jthe->jhef",
        query_blocks,
        numerator_delta,
        precision=HIGHEST,
        preferred_element_type=jnp.float32,
    )
    norm_before_delta = jnp.einsum(
        "jthf,jth->jhf",
        query_blocks,
        denominator_delta,
        precision=HIGHEST,
        preferred_element_type=jnp.float32,
    )
    leaving = (
        jnp.einsum("js,jhef->shef", member, before_delta, precision=HIGHEST),
        jnp.einsum("js,jhf->shf", member, norm_before_delta, precision=HIGHEST),
    )
    later_sums = entering(
        (leaving[0], leaving[1]),
        "ctx",
        add_pair,
        (jnp.zeros_like(leaving[0]), jnp.zeros_like(leaving[1])),
        True,
    )
    state_delta = jnp.einsum(
        "ji,jhef->ihef", earlier, before_delta, precision=HIGHEST
    ) + jnp.einsum("js,shef->jhef", member, later_sums[0], precision=HIGHEST)
    block_norm_delta = jnp.einsum(
        "ji,jhf->ihf", earlier, norm_before_delta, precision=HIGHEST
    ) + jnp.einsum("js,shf->jhf", member, later_sums[1], precision=HIGHEST)
    value_delta = value_delta + jnp.einsum(
        "jhef,jthf->jthe",
        state_delta,
        key_blocks,
        precision=HIGHEST,
        preferred_element_type=jnp.float32,
    )
    key_delta = (
        key_delta
        + jnp.einsum(
            "jhef,jthe->jthf",
            state_delta,
            value_blocks,
            precision=HIGHEST,
            preferred_element_type=jnp.float32,
        )
        + block_norm_delta[:, None]
    )
    query_in_delta, query_weight_delta, query_bias_delta = query_pull(
        rounded(query_delta).reshape(piece_rows, heads_here, 2 * HD)
    )
    key_in_delta, key_weight_delta, key_bias_delta = key_pull(
        rounded(key_delta).reshape(piece_rows, heads_here, 2 * HD)
    )
    mixed_delta = jnp.stack(
        [query_in_delta, key_in_delta, value_delta.reshape(piece_rows, heads_here, HD)], axis=1
    )
    mixed_delta = mixed_delta.astype(jnp.bfloat16).reshape(piece_rows, 3 * heads_here * HD)
    mixer_bias_delta = jnp.sum(mixed_delta.astype(jnp.float32), axis=0).reshape(3, heads_here * HD)
    mixer_delta = jnp.einsum(
        "td,tk->dk", first_rows, mixed_delta, preferred_element_type=jnp.float32
    ).reshape(model_width, 3, heads_here * HD)
    first_delta = lax.psum_scatter(
        jnp.einsum("tk,dk->td", mixed_delta, mixer_flat, preferred_element_type=jnp.float32).astype(
            jnp.bfloat16
        ),
        "tp",
        scatter_dimension=0,
        tiled=True,
    ).astype(jnp.float32)
    input_back, first_gain_part, first_bias_part = first_pull(first_delta)
    tokens_delta = middle_delta + input_back
    feature_weight_delta = jnp.stack([query_weight_delta, key_weight_delta])
    feature_bias_delta = jnp.stack([query_bias_delta, key_bias_delta])
    output_bias_part = jnp.sum(middle_delta, axis=0)
    outer_bias_part = jnp.sum(upstream, axis=0)
    summed = lax.psum(
        (
            mixer_delta,
            mixer_bias_delta,
            feature_weight_delta,
            feature_bias_delta,
            output_delta,
            inner_delta,
            inner_bias_delta,
            outer_delta,
            first_gain_part,
            first_bias_part,
            output_bias_part,
            second_gain_part,
            second_bias_part,
            outer_bias_part,
        ),
        ("dp", "ctx"),
    )
    shared = lax.psum((summed[8], summed[9], summed[10], summed[11], summed[12], summed[13]), "tp")
    return (
        result,
        tokens_delta,
        shared[0],
        shared[1],
        summed[0],
        summed[1],
        summed[2],
        summed[3],
        summed[4],
        shared[2],
        shared[3],
        shared[4],
        summed[5],
        summed[6],
        summed[7],
        shared[5],
    )


def solution(mesh):
    in_specs = (
        P(("dp", "ctx", "tp"), None),
        P(),
        P(),
        P(None, None, "tp"),
        P(None, "tp"),
        P(None, "tp", None, None),
        P(None, "tp", None),
        P("tp", None),
        P(),
        P(),
        P(),
        P(None, "tp"),
        P("tp"),
        P("tp", None),
        P(),
        P("dp", None),
        P(("dp", "ctx", "tp"), None),
    )
    out_specs = (
        P(("dp", "ctx", "tp"), None),
        P(("dp", "ctx", "tp"), None),
        P(),
        P(),
        P(None, None, "tp"),
        P(None, "tp"),
        P(None, "tp", None, None),
        P(None, "tp", None),
        P("tp", None),
        P(),
        P(),
        P(),
        P(None, "tp"),
        P("tp"),
        P("tp", None),
        P(),
    )
    return jax.shard_map(shards, mesh=mesh, in_specs=in_specs, out_specs=out_specs, check_vma=False)
```

profile of v0, /device:TPU:0, one launch (start us, length us, event | category | flops | bytes accessed | tf_op | source)
XLA Modules:
  0.0 1006.3 jit_solution(10132067115701984201)
XLA Ops:
  14.2 65.0 %all-gather.11.cloned.1.call-done = bf16[2048,768]{1,0:T(8,128)(2,1)} async-done(((bf16[512,768]{1,0:T(8,128)(2,1)}), bf16[2048,768]{1,0:T(8,128)(2,1)}) %all-gather.11.cloned.1.call-update) | async-done | bytes 3145744 | tf_op jit(solution)/shard_map/all_gather | solution.py:97
  79.2 3.9 add_convert_fusion
  84.5 2.9 fusion.124
  94.4 3.4 reshape_squeeze.3
  97.8 3.4 copy.124
  103.5 3.4 concatenate.19
  106.9 3.4 copy.107
  112.1 2.7 concatenate.18
  117.1 4.3 convert_reduce_fusion.3
  121.6 5.6 all-gather.4
  127.4 2.5 concatenate.22
  129.9 3.5 copy.115
  135.1 3.4 concatenate.21
  138.5 3.5 copy.114
  144.1 2.9 fusion.27
  147.0 7.0 all-gather
  154.0 6.5 while.34
  161.7 5.7 multiply_add_fusion.3
  169.4 2.5 fusion.81
  171.9 4.7 fusion.25
  176.7 2.9 fusion.125
  181.7 2.8 reshape.270
  184.6 3.7 fusion.127
  189.6 108.3 %reduce-scatter.5.cloned.1.call-done = f32[512,768]{1,0:T(8,128)} async-done(((f32[2048,768]{1,0:T(8,128)}), f32[512,768]{1,0:T(8,128)}) %reduce-scatter.5.cloned.1.call-update) | async-done | bytes 1572880 | tf_op jit(solution)/shard_map/reduce_scatter | solution.py:162
  303.6 62.3 %all-gather.13.cloned.1.call-done = bf16[2048,768]{1,0:T(8,128)(2,1)} async-done(((bf16[512,768]{1,0:T(8,128)(2,1)}), bf16[2048,768]{1,0:T(8,128)(2,1)}) %all-gather.13.cloned.1.call-update) | async-done | bytes 3145744 | tf_op jit(solution)/shard_map/all_gather | solution.py:173
  365.9 7.5 fusion.128
  373.4 56.1 %all-gather.15.cloned.1.call-done = bf16[2048,768]{1,0:T(8,128)(2,1)} async-done(((bf16[512,768]{1,0:T(8,128)(2,1)}), bf16[2048,768]{1,0:T(8,128)(2,1)}) %all-gather.15.cloned.1.call-update) | async-done | bytes 3145744 | tf_op jit(solution)/shard_map/all_gather | solution.py:187
  429.5 12.2 %convert_reduce_fusion = (f32[768]{0:T(1024)}, bf16[2048,768]{1,0:T(8,128)(2,1)S(1)}, bf16[2048,768]{1,0:T(8,128)(2,1)}) fusion(f32[2048,768]{1,0:T(8,128)} %fusion.128, f32[768]{0:T(1024)} %convert_element_type.136, bf16[2048,768]{1,0:T(8,128)(2,1)} %all-gather.15.cloned.1.call-done, bf16[768,768]{1,0:T(8,128)(2,1)S(1)} %copy-done), kind=kOutput, calls=%fused_computation.18 | convolution fusion | flops 2461531392 | bytes 16914432 | tf_op jit(solution)/shard_map/td,fd->tf/dot_general | solution.py:191
  443.4 4.6 fusion.129
  448.1 6.3 convolution_convert_fusion
  455.0 102.6 %reduce-scatter.9.cloned.1.call-done = f32[512,768]{1,0:T(8,128)} async-done(((f32[2048,768]{1,0:T(8,128)}), f32[512,768]{1,0:T(8,128)}) %reduce-scatter.9.cloned.1.call-update) | async-done | bytes 1572880 | tf_op jit(solution)/shard_map/reduce_scatter | solution.py:200
  557.6 2.6 multiply_reduce_fusion.1
  560.2 60.3 %reduce-scatter.7.cloned.1.call-done = bf16[512,768]{1,0:T(8,128)(2,1)} async-done(((bf16[2048,768]{1,0:T(8,128)(2,1)}), bf16[512,768]{1,0:T(8,128)(2,1)}) %reduce-scatter.7.cloned.1.call-update) | async-done | bytes 786448 | tf_op jit(solution)/shard_map/reduce_scatter | solution.py:179
  620.6 3.2 fusion.115
  629.5 60.4 %all-gather.17.cloned.1.call-done = bf16[2048,768]{1,0:T(8,128)(2,1)} async-done(((bf16[512,768]{1,0:T(8,128)(2,1)}), bf16[2048,768]{1,0:T(8,128)(2,1)}) %all-gather.17.cloned.1.call-update) | async-done | bytes 3145744 | tf_op jit(solution)/shard_map/all_gather | solution.py:209
  689.9 3.1 convolution_convert_fusion.2
  693.0 2.6 reshape.285
  695.6 5.2 multiply_reduce_fusion
  701.0 10.8 %fusion.23 = f32[32,3,128,64]{2,3,1,0:T(8,128)} fusion(f32[32,3,64,128]{3,0,2,1:T(8,128)S(1)} %copy-done.27, f32[32,64,3,64]{1,0,3,2:T(8,128)S(1)} %copy-done.24, f32[32,64,3]{1,2,0:T(4,128)S(1)} %copy-done.56), kind=kOutput, calls=%fused_computation.50 | convolution fusion | flops 604372992 | bytes 7888896 | tf_op jit(solution)/shard_map/jthe,jhef->jthf/dot_general | solution.py:239
  711.8 4.3 fusion.111
  717.6 5.2 all-gather.5
  722.8 2.9 fusion.19
  725.7 6.5 all-gather.2
  733.0 5.7 multiply_add_fusion.2
  738.7 4.8 fusion.15
  743.6 4.5 fusion.17
  748.1 4.4 select_convert_fusion
  756.5 4.9 bitcast_add_fusion
  767.2 3.7 fusion.119
  770.9 3.4 copy.180
  776.1 3.4 copy.181
  781.8 3.6 fusion.118
  785.5 3.2 copy.178
  790.9 3.6 copy.179
  797.4 4.9 fusion.113
  806.1 4.1 convolution_convert_fusion.1
  810.5 7.0 fusion.132
  817.5 4.1 fusion.131
  826.6 3.3 fusion.10
  830.0 39.3 %reduce-scatter.11.cloned.1.call-done = bf16[512,768]{1,0:T(8,128)(2,1)} async-done(((bf16[2048,768]{1,0:T(8,128)(2,1)}), bf16[512,768]{1,0:T(8,128)(2,1)}) %reduce-scatter.11.cloned.1.call-update) | async-done | bytes 786448 | tf_op jit(solution)/shard_map/reduce_scatter | solution.py:314
  875.3 26.5 %all-reduce = (f32[768]{0:T(1024)S(1)}, f32[768]{0:T(1024)S(1)}, f32[3,192]{1,0:T(4,128)}, f32[2,3,64]{2,1,0:T(4,128)S(1)}, f32[768]{0:T(1024)S(1)}, /*index=5*/...) all-reduce(f32[768]{0:T(1024)S(1)} %get-tuple-element.373, ...), channel_id=1, replica_groups=mesh['dp'=2,'ctx'=4,'tp'=4] {'dp','ctx'}, use_global_device_ids=true, to_apply=%region_32.33 | all-reduce | flops 6336 | bytes 50688 | tf_op jit(solution)/shard_map/psum | solution.py:328
  902.4 18.5 %all-reduce.2 = (f32[768]{0:T(1024)}, f32[768]{0:T(1024)}, f32[768]{0:T(1024)}, f32[768]{0:T(1024)}, f32[768]{0:T(1024)}, /*index=5*/f32[768]{0:T(1024)}) all-reduce(f32[768]{0:T(1024)S(1)} %get-tuple-element.404, f32[768]{0:T(1024)S(1)} %get-tuple-element.405, ...), channel_id=1, replica_groups=mesh['dp'=2,'ctx'=4,'tp'=4] {'tp'}, use_global_device_ids=true, to_apply=%region_33.34 | all-reduce | flops 4608 | bytes 36864 | tf_op jit(solution)/shard_map/psum | solution.py:347
  920.9 70.3 %all-reduce.5.cloned.1.call-done = (f32[768,3,192]{0,2,1:T(8,128)}, f32[2,3,64,64]{3,2,1,0:T(8,128)}, f32[192,768]{1,0:T(8,128)}, f32[768,768]{1,0:T(8,128)}, f32[768,768]{1,0:T(8,128)}) async-done(((f32[768,3,192]{0,2,1:T(8,128)}, f32[2,3,64,64]{3,2,1,0:T(8,128)}, f32[192,768]{1,0:T(8,128)}, f32[768,768]{1,0:T(8,128)}, f32[768,768]{1,0:T(8,128)}), (f32[768,3,192]{0,2,1:T(8,128)}, ...) | async-done | bytes 7176208 | tf_op jit(solution)/shard_map/psum | solution.py:328
  991.2 2.9 copy.256
  (337 shorter events, 94.9 us)
Async XLA Ops:
  7.2 422.3 %copy-start = (bf16[768,768]{1,0:T(8,128)(2,1)S(1)}, bf16[768,768]{1,0:T(8,128)(2,1)}, u32[]{:S(2)}) copy-start(bf16[768,768]{1,0:T(8,128)(2,1)} %param.34) | copy-start | bytes 3538948
  7.2 4.4 copy-start.2
  7.2 3.7 copy-start.88
  7.2 3.7 copy-start.89
  7.2 72.0 %all-gather.11.cloned.1.call-start = ((), (), s32[]{:S(2)}) async-start(), calls=%async_computation.4 | async-start | bytes 3932160 | tf_op jit(solution)/shard_map/all_gather | solution.py:97
  8.7 4.2 copy-start.85
  8.7 4.2 copy-start.90
  8.8 4.9 copy-start.75
  8.8 70.4 %copy-start.98 = (bf16[768,3,192]{0,2,1:T(8,128)(2,1)S(1)}, bf16[768,3,192]{0,2,1:T(8,128)(2,1)}, u32[]{:S(2)}) copy-start(bf16[768,3,192]{0,2,1:T(8,128)(2,1)} %param.24) | copy-start | bytes 2654212
  12.8 285.1 %reduce-scatter.5.cloned.1.call-start = ((), (), s32[]{:S(2)}) async-start(), calls=%async_computation.5 | async-start | bytes 7864320 | tf_op jit(solution)/shard_map/reduce_scatter | solution.py:162
  83.1 6.6 copy-start.34
  87.5 22.8 %copy-start.5 = (f32[2048,3,64]{0,2,1:T(8,128)}, f32[2048,3,64]{0,2,1:T(8,128)S(1)}, u32[]{:S(2)}) copy-start(f32[2048,3,64]{0,2,1:T(8,128)S(1)} %get-tuple-element.454) | copy-start | bytes 4718596
  117.1 10.1 %copy-start.11 = (f32[2048,3,64]{0,2,1:T(8,128)S(1)}, f32[2048,3,64]{0,2,1:T(8,128)}, u32[]{:S(2)}) copy-start(f32[2048,3,64]{0,2,1:T(8,128)} %get-tuple-element.448) | copy-start | bytes 4718596
  117.1 10.1 %copy-start.48 = (f32[2048,3]{0,1:T(4,128)S(1)}, f32[2048,3]{0,1:T(4,128)}, u32[]{:S(2)}) copy-start(f32[2048,3]{0,1:T(4,128)} %get-tuple-element.447) | copy-start | bytes 73732
  121.4 5.8 copy-start.59
  161.7 7.7 copy-start.71
  161.7 5.7 copy-start.36
  161.7 5.7 copy-start.37
  167.4 4.5 copy-start.26
  169.3 7.3 copy-start.57
  169.4 7.3 copy-start.100
  171.9 4.7 copy-start.61
  171.9 4.8 copy-start.20
  188.3 177.6 %all-gather.13.cloned.1.call-start = ((), (), s32[]{:S(2)}) async-start(), calls=%async_computation.6 | async-start | bytes 3932160 | tf_op jit(solution)/shard_map/all_gather | solution.py:173
  301.7 127.8 %all-gather.15.cloned.1.call-start = ((), (), s32[]{:S(2)}) async-start(), calls=%async_computation.8 | async-start | bytes 3932160 | tf_op jit(solution)/shard_map/all_gather | solution.py:187
  302.3 255.3 %reduce-scatter.9.cloned.1.call-start = ((), (), s32[]{:S(2)}) async-start(), calls=%async_computation.9 | async-start | bytes 7864320 | tf_op jit(solution)/shard_map/reduce_scatter | solution.py:200
  429.5 13.9 %copy-start.97 = (bf16[768,768]{1,0:T(8,128)(2,1)S(1)}, bf16[768,768]{1,0:T(8,128)(2,1)}, u32[]{:S(2)}) copy-start(bf16[768,768]{1,0:T(8,128)(2,1)} %param.32) | copy-start | bytes 3538948
  448.0 172.5 %reduce-scatter.7.cloned.1.call-start = ((), (), s32[]{:S(2)}) async-start(), calls=%async_computation.7 | async-start | bytes 3932160 | tf_op jit(solution)/shard_map/reduce_scatter | solution.py:179
  454.4 235.5 %all-gather.17.cloned.1.call-start = ((), (), s32[]{:S(2)}) async-start(), calls=%async_computation.10 | async-start | bytes 3932160 | tf_op jit(solution)/shard_map/all_gather | solution.py:209
  455.0 105.2 %copy-start.79 = (f32[512]{0:T(512)S(1)}, f32[512]{0:T(512)}, u32[]{:S(2)}) copy-start(f32[512]{0:T(512)} %copy-done.78) | copy-start | bytes 6148
  560.2 64.8 %copy-start.32 = (bf16[512,768]{1,0:T(8,128)(2,1)S(1)}, bf16[512,768]{1,0:T(8,128)(2,1)}, u32[]{:S(2)}) copy-start(bf16[512,768]{1,0:T(8,128)(2,1)} %param.37) | copy-start | bytes 2359300
  625.0 3.8 copy-start.49
  625.0 64.9 %copy-start.53 = (bf16[192,768]{1,0:T(8,128)(2,1)S(1)}, bf16[192,768]{1,0:T(8,128)(2,1)}, u32[]{:S(2)}) copy-start(bf16[192,768]{1,0:T(8,128)(2,1)} %param.28) | copy-start | bytes 884740
  626.2 243.1 %reduce-scatter.11.cloned.1.call-start = ((), (), s32[]{:S(2)}) async-start(), calls=%async_computation.11 | async-start | bytes 3932160 | tf_op jit(solution)/shard_map/reduce_scatter | solution.py:314
  692.9 7.9 copy-start.58
  693.0 7.9 copy-start.62
  695.6 5.3 copy-start.56
  695.6 5.4 copy-start.24
  695.6 5.4 copy-start.27
  701.0 10.8 %copy-start.23 = (bf16[32,64,3,128]{3,1,2,0:T(8,128)(2,1)S(1)}, bf16[32,64,3,128]{3,1,2,0:T(8,128)(2,1)}, u32[]{:S(2)}) copy-start(bf16[32,64,3,128]{3,1,2,0:T(8,128)(2,1)} %copy-done.22) | copy-start | bytes 4718596
  716.1 9.5 copy-start.28
  725.7 7.3 copy-start.87
  733.0 5.7 copy-start.13
  738.7 4.8 copy-start.21
  743.5 4.5 copy-start.25
  743.5 4.5 copy-start.84
  748.1 4.5 copy-start.39
  748.1 4.5 copy-start.54
  797.4 4.9 copy-start.51
  810.2 181.0 %all-reduce.5.cloned.1.call-start = ((), (), s32[]{:S(2)}) async-start(), calls=%async_computation.12 | async-start | bytes 14548992 | tf_op jit(solution)/shard_map/psum | solution.py:328
  810.5 7.1 copy-start.96
  810.5 7.1 copy-start.103
  817.5 4.2 copy-start.17
  817.5 4.2 copy-start.35
  817.5 7.2 copy-start.38
  829.8 39.5 %copy-start.68 = (f32[768]{0:T(1024)S(1)}, f32[768]{0:T(1024)}, u32[]{:S(2)}) copy-start(f32[768]{0:T(1024)} %copy-done.67) | copy-start | bytes 9220
  829.8 39.5 %copy-start.70 = (f32[512]{0:T(512)S(1)}, f32[512]{0:T(512)}, u32[]{:S(2)}) copy-start(f32[512]{0:T(512)} %copy-done.69) | copy-start | bytes 6148
  829.9 41.3 %copy-start.77 = (f32[512]{0:T(512)S(1)}, f32[512]{0:T(512)}, u32[]{:S(2)}) copy-start(f32[512]{0:T(512)} %copy-done.76) | copy-start | bytes 6148
  829.9 41.3 %copy-start.74 = (f32[512]{0:T(512)S(1)}, f32[512]{0:T(512)}, u32[]{:S(2)}) copy-start(f32[512]{0:T(512)} %copy-done.73) | copy-start | bytes 6148
  830.0 43.3 %copy-start.19 = (f32[512,768]{1,0:T(8,128)S(1)}, f32[512,768]{1,0:T(8,128)}, u32[]{:S(2)}) copy-start(f32[512,768]{1,0:T(8,128)} %copy-done.18) | copy-start | bytes 4718596
  869.3 3.9 copy-start.31
  869.3 4.0 copy-start.33
  991.2 4.5 copy-start.43
  995.7 3.9 copy-start.1
  (49 other events, 106.0 us)
Sparse Core Ops, SparseCore 0:
  12.9 66.1 all-gather.10
  188.4 109.4 reduce-scatter.4
  301.8 64.0 all-gather.12
  367.3 62.1 all-gather.14
  448.2 109.3 reduce-scatter.8
  559.8 60.7 reduce-scatter.6
  626.3 63.5 all-gather.16
  810.4 58.9 reduce-scatter.10
  874.4 116.7 all-reduce.4
where the time goes:
time: 1020 us; the launch traced here: 1010 us
  waiting for transfers between devices  625 us (61%)
  matrix products  136 us (13%)
  local copies, waits for them, and re-layouts  86.1 us (8%)
  other arithmetic  72.6 us (7%)
  blocking collectives  69.3 us (7%)
  between operations  15.4 us (2%)
    reduce_scatter x1, waiting for transfers between devices, shards(): lax.psum_scatter(jnp.dot(attended_low, output_weight, preferred_element_t...  108 us
    reduce_scatter x1, waiting for transfers between devices, shards(): lax.psum_scatter(jnp.einsum('tf,df->td', hidden_low, inner_weight, prefer...  103 us
    psum x1, waiting for transfers between devices, shards(): lax.psum((mixer_delta, mixer_bias_delta, feature_weight_delta, feature_bi...  70.3 us
    all_gather x1, waiting for transfers between devices, shards(): first_rows = lax.all_gather(first_low, 'tp', axis=0, tiled=True)  65 us
    all_gather x1, waiting for transfers between devices, shards(): second_rows = lax.all_gather(second_low, 'tp', axis=0, tiled=True)  62.3 us
    all_gather x1, waiting for transfers between devices, shards(): middle_rows = lax.all_gather(middle_low, 'tp', axis=0, tiled=True)  60.4 us
    reduce_scatter x1, waiting for transfers between devices, shards(): lax.psum_scatter(jnp.dot(activated, outer_weight, preferred_element_type=...  60.3 us
    all_gather x1, waiting for transfers between devices, shards(): upstream_rows = lax.all_gather(cotangent, 'tp', axis=0, tiled=True)  56.1 us
  transfers between devices with their start and end apart: 9, of which 9 were waited for; matrix products, arithmetic and copies ran while one was open for 5% of the time, Pallas kernels for 0%

commit v1 on v0

v1 whole, which is shorter than its diff:
```python
import jax
import jax.numpy as jnp
from jax import lax
from jax.sharding import PartitionSpec as P

HD = 64
BLOCK = 64
CHUNK = 256
EPSILON = 1e-05
F32 = jnp.float32
BF16 = jnp.bfloat16
ALL = ("dp", "ctx", "tp")


def ein(spec, a, b):
    return jnp.einsum(spec, a, b, preferred_element_type=F32)


def layer_norm(v, gain, offset):
    c = v - jnp.mean(v, axis=-1, keepdims=True)
    r = lax.rsqrt(jnp.mean(c * c, axis=-1, keepdims=True) + EPSILON)
    n = c * r
    return n * gain + offset, n, r


def layer_norm_back(e, n, r, gain):
    m = e * gain
    back = r * (
        m - jnp.mean(m, axis=-1, keepdims=True) - n * jnp.mean(m * n, axis=-1, keepdims=True)
    )
    return back, jnp.sum(e * n, axis=0), jnp.sum(e, axis=0)


def gelu_parts(s):
    t = jnp.tanh(0.7978845608028654 * (s + 0.044715 * s * s * s))
    slope = 0.7978845608028654 * (1.0 + 3.0 * 0.044715 * s * s)
    return 0.5 * s * (1.0 + t), 0.5 * (1.0 + t) + 0.5 * s * (1.0 - t * t) * slope


def feature_map(q, weight, offset):
    u = ein("thd,hde->the", q, weight) + offset
    up, down = jax.nn.softmax(u, axis=-1), jax.nn.softmax(-u, axis=-1)
    return up, down, jnp.concatenate([up, down], axis=-1).astype(BF16)


def feature_back(delta, up, down, q, weight):
    d, dd = delta[..., :HD], delta[..., HD:]
    du = up * (d - jnp.sum(up * d, axis=-1, keepdims=True)) - down * (
        dd - jnp.sum(down * dd, axis=-1, keepdims=True)
    )
    low = du.astype(BF16)
    return ein("the,hde->thd", low, weight), ein("thd,the->hde", q, low), jnp.sum(du, axis=0)


def merge_heads(gathered):
    tp, rows, three, width = gathered.shape
    return gathered.transpose(1, 2, 0, 3).reshape(rows, three, tp * width)


def shards(
    tokens,
    first_gain,
    first_bias,
    mixer_weight,
    mixer_bias,
    feature_weight,
    feature_bias,
    output_weight,
    output_bias,
    second_gain,
    second_bias,
    inner_weight,
    inner_bias,
    outer_weight,
    outer_bias,
    block_owner,
    cotangent,
):
    rows, width = tokens.shape
    n_tp, n_ctx = lax.axis_size("tp"), lax.axis_size("ctx")
    n_plane = lax.axis_size("dp") * n_ctx
    plane = lax.axis_index("dp") * n_ctx + lax.axis_index("ctx")
    heads_here = mixer_weight.shape[2] // HD
    heads = heads_here * n_tp
    mine = lax.axis_index("ctx") * n_tp + lax.axis_index("tp")

    mixer_t = mixer_weight.transpose(1, 2, 0).reshape(-1, width)
    sizes = [w.shape[0] for w in (mixer_t, output_weight, inner_weight, outer_weight)]
    pack = jnp.concatenate([mixer_t, output_weight, inner_weight, outer_weight], axis=0)
    part = pack.shape[0] // n_plane
    piece = lax.dynamic_slice_in_dim(pack, plane * part, part, 0)
    full = lax.all_gather(piece, ALL, axis=0, tiled=True)
    full = full.reshape(n_plane, n_tp, part, width).transpose(1, 0, 2, 3).reshape(n_tp, -1, width)
    cuts = [0]
    for s in sizes:
        cuts.append(cuts[-1] + s)
    mixer_all, output_all, inner_all, outer_all = [
        full[:, a:b] for a, b in zip(cuts[:-1], cuts[1:])
    ]
    small = jnp.concatenate(
        [feature_weight.reshape(-1), mixer_bias.reshape(-1), feature_bias.reshape(-1), inner_bias]
    )
    small = lax.all_gather(small, "tp")
    cut = feature_weight.size
    feature_all = (
        small[:, :cut].reshape(n_tp, 2, heads_here, HD, HD).transpose(1, 0, 2, 3, 4)
    ).reshape(2, heads, HD, HD)
    mixer_bias_all = small[:, cut : cut + mixer_bias.size].astype(F32).reshape(n_tp, -1)
    cut += mixer_bias.size
    feature_bias_all = (
        small[:, cut : cut + feature_bias.size]
        .astype(F32)
        .reshape(n_tp, 2, heads_here, HD)
        .transpose(1, 0, 2, 3)
        .reshape(2, heads, HD)
    )
    cut += feature_bias.size
    inner_bias_all = small[:, cut:].astype(F32)

    x = tokens.astype(F32)
    gain1, gain2 = first_gain.astype(F32), second_gain.astype(F32)
    h1, n1, r1 = layer_norm(x, gain1, first_bias.astype(F32))
    h1 = h1.astype(BF16)
    mix = ein("td,skd->tsk", h1, mixer_all) + mixer_bias_all
    mix = mix.astype(BF16).reshape(rows, n_tp, 3, heads_here, HD).transpose(2, 0, 1, 3, 4)
    mix = mix.reshape(3, rows, heads, HD)
    q, k, v = mix[0], mix[1], mix[2]
    q_up, q_down, phi_q = feature_map(q, feature_all[0], feature_bias_all[0])
    k_up, k_down, phi_k = feature_map(k, feature_all[1], feature_bias_all[1])

    chunk = min(CHUNK, rows)
    chunks = rows // chunk
    pq = phi_q.reshape(chunks, chunk, heads, 2 * HD)
    pk = phi_k.reshape(chunks, chunk, heads, 2 * HD)
    vc = v.reshape(chunks, chunk, heads, HD)
    causal = jnp.arange(chunk)[:, None] >= jnp.arange(chunk)[None, :]
    state = ein("jthe,jthf->jhef", vc, pk)
    norm = jnp.sum(pk.astype(F32), axis=1)
    both = jnp.concatenate([state, norm[:, :, None]], axis=2)
    owners = block_owner[0].reshape(n_tp, -1)[:, 0]
    order = jnp.arange(n_ctx * n_tp)
    same = jnp.tile(owners, n_ctx) == jnp.tile(owners, n_ctx)[mine]

    def prefix(totals, reach):
        everything = lax.all_gather(totals.astype(BF16), ("ctx", "tp")).astype(F32)
        return jnp.einsum("s,shef->hef", reach.astype(F32), everything, precision="highest")

    def running(blocks, start, reverse):
        out = [None] * chunks
        acc = start
        for j in reversed(range(chunks)) if reverse else range(chunks):
            out[j] = acc
            acc = acc + blocks[j]
        return jnp.stack(out)

    before = running(both, prefix(jnp.sum(both, axis=0), same & (order < mine)), False)
    before = before.astype(BF16)
    scores = ein("jthf,jshf->jhts", pq, pk)
    a_low = jnp.where(causal, scores, 0.0).astype(BF16)
    v_one = jnp.concatenate([vc, jnp.ones(vc.shape[:-1] + (1,), BF16)], axis=-1)
    num = ein("jthf,jhef->jthe", pq, before) + ein("jhts,jshe->jthe", a_low, v_one)
    num, den = num[..., :HD], num[..., HD:]
    o = num / den
    o_low = o.astype(BF16)
    o_flat = o_low.reshape(rows, n_tp, heads_here * HD)
    x2 = x + ein("tsk,skd->td", o_flat, output_all) + output_bias.astype(F32)
    h2, n2, r2 = layer_norm(x2, gain2, second_bias.astype(F32))
    h2 = h2.astype(BF16)
    f = ein("td,sdf->tsf", h2, inner_all) + inner_bias_all
    a, slope = gelu_parts(f)
    a = a.astype(BF16)
    result = (x2 + ein("tsf,sfd->td", a, outer_all) + outer_bias.astype(F32)).astype(BF16)

    g = cotangent.astype(F32)
    d_outer = ein("tsf,td->sfd", a, cotangent)
    df = (ein("td,sfd->tsf", cotangent, outer_all) * slope).astype(BF16)
    d_inner_bias = jnp.sum(df.astype(F32), axis=0)
    d_inner = ein("td,tsf->sdf", h2, df)
    e2 = ein("tsf,sdf->td", df, inner_all)
    back2, d_gain2, d_bias2 = layer_norm_back(e2, n2, r2, gain2)
    dx2 = g + back2
    big_g = dx2.astype(BF16)
    d_output = ein("tsk,td->skd", o_flat, big_g)
    do = ein("td,skd->tsk", big_g, output_all).astype(BF16).astype(F32)
    do = do.reshape(chunks, chunk, heads, HD)
    dnum = do / den
    dden = -jnp.sum(do * o, axis=-1, keepdims=True) / den
    dne = jnp.concatenate([dnum, dden], axis=-1).astype(BF16)
    da = ein("jthe,jshe->jhts", dne, v_one)
    da_low = jnp.where(causal, da, 0.0).astype(BF16)
    d_both = ein("jthe,jthf->jhef", dne, pq)
    after = running(d_both, prefix(jnp.sum(d_both, axis=0), same & (order > mine)), True)
    after = after.astype(BF16)
    dphi_q = ein("jhts,jshf->jthf", da_low, pk) + ein("jthe,jhef->jthf", dne, before)
    dphi_k = ein("jhts,jthf->jshf", da_low, pq) + ein("jthe,jhef->jthf", v_one, after)
    dv = ein("jhts,jthe->jshe", a_low, dne[..., :HD]) + ein("jthf,jhef->jthe", pk, after[:, :, :HD])
    dphi_q = dphi_q.reshape(rows, heads, 2 * HD)
    dphi_k = dphi_k.reshape(rows, heads, 2 * HD)
    dq, d_fq, d_fbq = feature_back(dphi_q, q_up, q_down, q, feature_all[0])
    dk, d_fk, d_fbk = feature_back(dphi_k, k_up, k_down, k, feature_all[1])
    dmix = jnp.stack([dq, dk, dv.reshape(rows, heads, HD)], axis=1).astype(BF16)
    dmix = dmix.reshape(rows, 3, n_tp, heads_here * HD).transpose(0, 2, 1, 3)
    dmix = dmix.reshape(rows, n_tp, -1)
    d_mixer_bias = jnp.sum(dmix.astype(F32), axis=0)
    d_mixer = ein("tsk,td->skd", dmix, h1)
    e1 = ein("tsk,skd->td", dmix, mixer_all)
    back1, d_gain1, d_bias1 = layer_norm_back(e1, n1, r1, gain1)
    tokens_gradient = dx2 + back1

    big = jnp.concatenate([d_mixer, d_output, d_inner, d_outer], axis=1).astype(BF16)
    big = big.reshape(n_tp, n_plane, part, width).transpose(1, 0, 2, 3).reshape(-1, width)
    big = lax.psum_scatter(big, ("dp", "ctx"), scatter_dimension=0, tiled=True)
    big = lax.psum_scatter(big, "tp", scatter_dimension=0, tiled=True)
    big = lax.all_gather(big, ("dp", "ctx"), axis=0, tiled=True).astype(F32)
    d_mixer, d_output, d_inner, d_outer = [big[a:b] for a, b in zip(cuts[:-1], cuts[1:])]
    d_mixer = d_mixer.reshape(3, heads_here * HD, width).transpose(2, 0, 1)
    per_tp = jnp.concatenate(
        [
            jnp.stack([d_fq, d_fk]).reshape(2, n_tp, -1).transpose(1, 0, 2).reshape(n_tp, -1),
            d_mixer_bias,
            jnp.stack([d_fbq, d_fbk]).reshape(2, n_tp, -1).transpose(1, 0, 2).reshape(n_tp, -1),
            d_inner_bias,
        ],
        axis=1,
    )
    shared = jnp.stack(
        [d_gain1, d_bias1, jnp.sum(dx2, axis=0), d_gain2, d_bias2, jnp.sum(g, axis=0)]
    )
    total = lax.psum(jnp.concatenate([per_tp.reshape(-1), shared.reshape(-1)]), ALL)
    shared = total[per_tp.size :].reshape(6, width)
    own = lax.dynamic_slice_in_dim(
        total[: per_tp.size].reshape(n_tp, -1), lax.axis_index("tp"), 1, 0
    )[0]
    cut = feature_weight.size
    d_feature = own[:cut].reshape(feature_weight.shape)
    d_mixer_bias = own[cut : cut + mixer_bias.size].reshape(mixer_bias.shape)
    cut += mixer_bias.size
    d_feature_bias = own[cut : cut + feature_bias.size].reshape(feature_bias.shape)
    d_inner_bias = own[cut + feature_bias.size :]
    return (
        result,
        tokens_gradient,
        shared[0],
        shared[1],
        d_mixer,
        d_mixer_bias,
        d_feature,
        d_feature_bias,
        d_output,
        shared[2],
        shared[3],
        shared[4],
        d_inner,
        d_inner_bias,
        d_outer,
        shared[5],
    )


def solution(mesh):
    in_specs = (
        P(("dp", "ctx", "tp"), None),
        P(),
        P(),
        P(None, None, "tp"),
        P(None, "tp"),
        P(None, "tp", None, None),
        P(None, "tp", None),
        P("tp", None),
        P(),
        P(),
        P(),
        P(None, "tp"),
        P("tp"),
        P("tp", None),
        P(),
        P("dp", None),
        P(("dp", "ctx", "tp"), None),
    )
    out_specs = (
        P(("dp", "ctx", "tp"), None),
        P(("dp", "ctx", "tp"), None),
        P(),
        P(),
        P(None, None, "tp"),
        P(None, "tp"),
        P(None, "tp", None, None),
        P(None, "tp", None),
        P("tp", None),
        P(),
        P(),
        P(),
        P(None, "tp"),
        P("tp"),
        P("tp", None),
        P(),
    )
    return jax.shard_map(shards, mesh=mesh, in_specs=in_specs, out_specs=out_specs, check_vma=False)
```

time: 1020 us -> 596 us (0.58)
  waiting for transfers between devices: 625 us -> 373 us
  blocking collectives: 69.3 us -> 0 us
  other arithmetic: 72.6 us -> 25.4 us
  matrix products: 136 us -> 94.2 us
    reduce_scatter x4 -> x2, waiting for transfers between devices: 311 us -> 126 us  [the longest x1 92.7 us: shards(): big = lax.psum_scatter(big, ('dp', 'ctx'), scatter_dimension=0, tiled=True)]
    all_gather x4, waiting for transfers between devices: 244 us -> 109 us  [the longest x1 64.3 us: shards(): full = lax.all_gather(piece, ALL, axis=0, tiled=True)]
    dot_general x40 -> x30, matrix products: 136 us -> 83.7 us  [the longest x28 76.1 us: ein(): return jnp.einsum(spec, a, b, preferred_element_type=F32)]
    psum x2 -> x0, blocking collectives: 45 us -> none  [the longest x1 26.5 us: shards(): lax.psum((mixer_delta, mixer_bias_delta, feature_weight_delta, feature_bi...]
    unnamed x9, waiting for transfers between devices: 0.65 us -> 39.1 us
    reduce_sum x17 -> x8, other arithmetic: 39.7 us -> 8.16 us  [the longest x1 2.88 us: shards(): norm = jnp.sum(pk.astype(F32), axis=1)]
    psum x1, waiting for transfers between devices: 70.3 us -> 98.7 us  [shards(): lax.psum(jnp.concatenate([per_tp.reshape(-1), shared.reshape(-1)]), ALL)]
    all_gather x4 -> x0, blocking collectives: 24.3 us -> none  [entering(): everything = jax.tree.map(lambda part: lax.all_gather(part, axis), x)]
  transfers between devices with their start and end apart: 9 -> 8, of which waited for: 9 -> 7; matrix products, arithmetic and copies ran while one was open for 5% -> 14% of each run, Pallas kernels for 0% -> 0%
where the time goes in v1:
time: 596 us; the launch traced here: 587 us
  waiting for transfers between devices  373 us (63%)
  matrix products  94.2 us (16%)
  local copies, waits for them, and re-layouts  76.2 us (13%)
  other arithmetic  25.4 us (4%)
  between operations  17.8 us (3%)
    psum x1, waiting for transfers between devices, shards(): lax.psum(jnp.concatenate([per_tp.reshape(-1), shared.reshape(-1)]), ALL)  98.7 us
    reduce_scatter x1, waiting for transfers between devices, shards(): big = lax.psum_scatter(big, ('dp', 'ctx'), scatter_dimension=0, tiled=True)  92.7 us
    dot_general x28, matrix products, ein(): return jnp.einsum(spec, a, b, preferred_element_type=F32)  76.1 us
    all_gather x1, waiting for transfers between devices, shards(): full = lax.all_gather(piece, ALL, axis=0, tiled=True)  64.3 us
    all_gather x2, waiting for transfers between devices, prefix(): everything = lax.all_gather(totals.astype(BF16), ('ctx', 'tp')).astype(F32)  45.1 us
    unnamed x9, waiting for transfers between devices  39.1 us
    reduce_scatter x1, waiting for transfers between devices, shards(): big = lax.psum_scatter(big, 'tp', scatter_dimension=0, tiled=True)  33 us
    unnamed x178, local copies, waits for them, and re-layouts  17.9 us
  transfers between devices with their start and end apart: 8, of which 7 were waited for; matrix products, arithmetic and copies ran while one was open for 14% of the time, Pallas kernels for 0%

profile of v1, /device:TPU:0, one launch (start us, length us, event | category | flops | bytes accessed | tf_op | source)
XLA Modules:
  0.0 587.1 jit_solution(1276671653266649449)
XLA Ops:
  10.6 1.2 dynamic-slice
  14.7 2.5 fusion.111
  17.9 39.0 %all-reduce.7.cloned.1.call-done = bf16[105216]{0:T(1024)(128)(2,1)} async-done(((bf16[105216]{0:T(1024)(128)(2,1)}), bf16[105216]{0:T(1024)(128)(2,1)}) %all-reduce.7.cloned.1.call-update) | async-done | bytes 210448
  56.9 1.2 reshape.293
  60.3 64.3 %all-gather.8.cloned.1.call-done = bf16[9216,768]{1,0:T(8,128)(2,1)} async-done(((bf16[288,768]{1,0:T(8,128)(2,1)}), bf16[9216,768]{1,0:T(8,128)(2,1)}) %all-gather.8.cloned.1.call-update) | async-done | bytes 14155792 | tf_op jit(solution)/shard_map/all_gather | solution.py:92
  124.6 6.8 %copy.78 = bf16[8,4,288,768]{3,2,0,1:T(8,128)(2,1)S(1)} copy(bf16[8,4,288,768]{3,2,1,0:T(8,128)(2,1)} %bitcast.268) | data formatting | bytes 28311552 | tf_op jit(solution)/shard_map/reshape | solution.py:93
  131.4 2.2 add_convert_fusion
  133.7 2.7 copy-done.3
  137.7 1.9 fusion.176
  139.7 2.6 fusion.177
  142.6 2.1 copy.83
  144.9 2.1 copy.82
  147.0 2.9 convert_reduce_fusion.2
  154.6 3.2 fusion.174
  158.0 2.3 copy.88
  160.3 2.8 fusion.175
  163.2 2.1 copy.87
  165.3 2.8 pad_maximum_fusion.2
  168.1 2.6 select_convert_fusion.1
  170.7 26.1 %all-gather.12.cloned.1.call-done = bf16[192,65,128]{2,1,0:T(8,128)(2,1)} async-done(((bf16[12,65,128]{2,1,0:T(8,128)(2,1)}), bf16[192,65,128]{2,1,0:T(8,128)(2,1)}) %all-gather.12.cloned.1.call-update) | async-done | bytes 3194896 | tf_op jit(solution)/shard_map/all_gather | solution.py:145
  196.8 3.8 fusion.30
  204.5 1.1 copy-done.5
  205.8 1.7 copy.92
  207.5 2.4 reshape.274
  210.0 2.5 fusion.178
  212.9 5.6 fusion.26
  218.6 6.9 %convert_reduce_fusion = (f32[4,768]{1,0:T(4,128)}, bf16[512,4,768]{2,0,1:T(8,128)(2,1)S(1)}) fusion(f32[512,4,768]{2,0,1:T(8,128)S(1)} %fusion.26, f32[4,768]{1,0:T(4,128)S(1)} %slice_convert_fusion, bf16[512,768]{1,0:T(8,128)(2,1)S(1)} %copy-done.41, bf16[4,2304,768]{2,1,0:T(8,128)(2,1)S(1)} %bitcast.265), kind=kOutput, calls=%fused_computation.23 | convolution fusion | flops 2450519040 | bytes 14966784 | tf_op jit(solution)/shard_map/td,sfd->tsf/dot_general | solution.py:16
  225.4 3.0 fusion.63
  229.2 2.0 fusion.90
  231.2 3.1 reshape.291
  234.3 2.4 multiply_reduce_fusion.4
  236.7 1.2 fusion.140
  237.9 2.1 fusion.179
  240.1 2.4 select_convert_fusion
  242.6 1.2 fusion.186
  245.8 1.9 fusion.3
  247.8 1.2 fusion.181
  249.0 1.3 convolution_convert_fusion.5
  250.6 1.8 convolution_convert_fusion.2
  252.8 1.8 fusion.188
  254.7 2.5 fusion.187
  257.2 4.5 convert_bitcast_fusion
  261.7 5.4 convolution_convert_fusion
  267.2 19.0 %all-gather.14.cloned.1.call-done = bf16[192,65,128]{2,1,0:T(8,128)(2,1)} async-done(((bf16[12,65,128]{2,1,0:T(8,128)(2,1)}), bf16[192,65,128]{2,1,0:T(8,128)(2,1)}) %all-gather.14.cloned.1.call-update) | async-done | bytes 3194896 | tf_op jit(solution)/shard_map/all_gather | solution.py:145
  286.1 3.8 fusion.28
  290.1 1.3 copy-done.22
  293.0 1.4 stack.82
  294.4 2.6 add_bitcast_fusion
  298.4 1.6 fusion.1
  300.1 1.2 fusion.180
  304.7 2.3 convolution_convert_fusion.1
  309.6 5.6 copy.108
  317.6 1.5 fusion.127
  320.1 1.8 fusion.124
  322.3 92.7 %reduce-scatter.3.cloned.1.call-done = bf16[1152,768]{1,0:T(8,128)(2,1)} async-done(((bf16[9216,768]{1,0:T(8,128)(2,1)}), bf16[1152,768]{1,0:T(8,128)(2,1)}) %reduce-scatter.3.cloned.1.call-update) | async-done | bytes 1769488 | tf_op jit(solution)/shard_map/reduce_scatter | solution.py:212
  415.9 6.2 %fusion.60 = (f32[768]{0:T(1024)S(1)}, f32[512]{0:T(512)S(1)}, f32[512]{0:T(512)S(1)}, f32[768]{0:T(1024)S(1)}, f32[512,768,1]{1,0,2:T(8,128)}) fusion(bf16[512,768]{1,0:T(8,128)(2,1)S(1)} %copy-done.14, f32[512]{0:T(512)S(1)} %copy-done.62, f32[512]{0:T(512)S(1)} %copy-done.49, f32[768]{0:T(1024)S(1)} %copy-done.52, bf16[512,4,576]{0,2,1:T(8,128)(2,1)} %bitcast.289, ...), kind=kOutput, calls=%fused_computation.83 | convolution fusion | flops 1815868928 | bytes 8274944 | tf_op jit(solution)/shard_map/tsk,skd->td/dot_general | solution.py:16
  423.4 33.0 %reduce-scatter.5.cloned.1.call-done = bf16[288,768]{1,0:T(8,128)(2,1)} async-done(((bf16[1152,768]{1,0:T(8,128)(2,1)}), bf16[288,768]{1,0:T(8,128)(2,1)}) %reduce-scatter.5.cloned.1.call-update) | async-done | bytes 442384 | tf_op jit(solution)/shard_map/reduce_scatter | solution.py:213
  456.5 9.5 %fusion.65 = bf16[512,768]{1,0:T(8,128)(2,1)} fusion(f32[512,768]{1,0:T(8,128)} %copy-done.20, bf16[4,2304,768]{2,1,0:T(8,128)(2,1)} %bitcast.262, f32[768]{0:T(1024)S(1)} %convert_element_type.145, f32[512,4,768]{2,0,1:T(8,128)} %copy-done.73, f32[4,768]{1,0:T(4,128)S(1)} %copy-done.54), kind=kOutput, calls=%fused_computation.97 | convolution fusion | flops 2432827392 | bytes 13384704 | tf_op jit(solution)/shard_map/tsf,sfd->td/dot_general | solution.py:16
  466.0 1.7 fusion.59
  467.7 98.7 %all-reduce.5.cloned.1.call-done = f32[109824]{0:T(1024)} async-done(((f32[109824]{0:T(1024)}), f32[109824]{0:T(1024)}) %all-reduce.5.cloned.1.call-update) | async-done | bytes 439312 | tf_op jit(solution)/shard_map/psum | solution.py:229
  571.0 1.4 fusion.171
  572.4 1.8 slice.221
  574.2 2.6 slice.219
  576.9 2.5 fusion.169
  (294 shorter events, 41.6 us)
Async XLA Ops:
  8.0 48.9 %all-reduce.7.cloned.1.call-start = ((), (), s32[]{:S(2)}) async-start(), calls=%async_computation.9 | async-start | bytes 421888
  14.7 109.9 %all-gather.8.cloned.1.call-start = ((), (), s32[]{:S(2)}) async-start(), calls=%async_computation.2 | async-start | bytes 14598144 | tf_op jit(solution)/shard_map/all_gather | solution.py:92
  14.7 2.6 copy-start.66
  14.7 2.6 copy-start.67
  14.7 2.6 copy-start.12
  17.2 179.6 %all-gather.12.cloned.1.call-start = ((), (), s32[]{:S(2)}) async-start(), calls=%async_computation.7 | async-start | bytes 3760128 | tf_op jit(solution)/shard_map/all_gather | solution.py:145
  17.3 114.1 %copy-start.50 = (f32[768]{0:T(1024)}, f32[768]{0:T(1024)S(1)}, u32[]{:S(2)}) copy-start(f32[768]{0:T(1024)S(1)} %convert_element_type.129) | copy-start | bytes 9220
  17.3 114.1 %copy-start.64 = (f32[768]{0:T(1024)}, f32[768]{0:T(1024)S(1)}, u32[]{:S(2)}) copy-start(f32[768]{0:T(1024)S(1)} %convert_element_type.130) | copy-start | bytes 9220
  17.5 113.9 %copy-start.48 = (f32[512]{0:T(512)}, f32[512]{0:T(512)S(1)}, u32[]{:S(2)}) copy-start(f32[512]{0:T(512)S(1)} %broadcast_multiply_fusion.5) | copy-start | bytes 6148
  17.9 113.5 %copy-start.60 = (f32[512]{0:T(512)}, f32[512]{0:T(512)S(1)}, u32[]{:S(2)}) copy-start(f32[512]{0:T(512)S(1)} %add_rsqrt_fusion.1) | copy-start | bytes 6148
  59.0 78.7 %copy-start.63 = (f32[12,64]{1,0:T(8,128)}, f32[12,64]{1,0:T(8,128)S(1)}, u32[]{:S(2)}) copy-start(f32[12,64]{1,0:T(8,128)S(1)} %add.177) | copy-start | bytes 9220
  60.3 79.4 %copy-start.43 = (bf16[1,4,3,64,64]{3,4,2,1,0:T(8,128)(2,1)}, bf16[1,4,3,64,64]{3,4,2,1,0:T(8,128)(2,1)S(1)}, u32[]{:S(2)}) copy-start(bf16[1,4,3,64,64]{3,4,2,1,0:T(8,128)(2,1)S(1)} %get-tuple-element.76) | copy-start | bytes 294916
  131.4 5.0 copy-start.3
  149.9 2.9 copy-start.68
  149.9 2.9 copy-start.69
  149.9 2.9 copy-start.70
  149.9 3.5 copy-start.46
  150.3 7.5 %copy-start.17 = (f32[2,12,64,128]{3,2,1,0:T(8,128)}, f32[2,12,64,128]{3,2,1,0:T(8,128)S(1)}, u32[]{:S(2)}) copy-start(f32[2,12,64,128]{3,2,1,0:T(8,128)S(1)} %fusion.164) | copy-start | bytes 2359300
  151.2 134.9 %all-gather.14.cloned.1.call-start = ((), (), s32[]{:S(2)}) async-start(), calls=%async_computation.8 | async-start | bytes 3760128 | tf_op jit(solution)/shard_map/all_gather | solution.py:145
  153.5 108.2 %copy-start.53 = (f32[4,768]{1,0:T(4,128)}, f32[4,768]{1,0:T(4,128)S(1)}, u32[]{:S(2)}) copy-start(f32[4,768]{1,0:T(4,128)S(1)} %slice_convert_fusion) | copy-start | bytes 36868
  158.0 2.3 copy-start.29
  168.1 32.7 %copy-start = (bf16[2,256,12,128]{3,1,2,0:T(8,128)(2,1)}, bf16[2,256,12,128]{3,1,2,0:T(8,128)(2,1)S(1)}, u32[]{:S(2)}) copy-start(bf16[2,256,12,128]{3,1,2,0:T(8,128)(2,1)S(1)} %pad_maximum_fusion.2) | copy-start | bytes 4718596
  196.8 3.8 copy-start.18
  205.8 4.2 copy-start.13
  210.0 2.6 copy-start.26
  210.0 8.5 %slice-start = ((s8[14155776]{0:T(1024)(128)(4,1)}), s8[4194304]{0:T(1024)(128)(4,1)S(1)}, s32[]{:S(2)}) async-start(s8[14155776]{0:T(1024)(128)(4,1)} %bitcast.263), calls=%async_computation.10 | async-start | bytes 8388608
  212.5 15.9 %copy-start.20 = (f32[512,768]{1,0:T(8,128)}, f32[512,768]{1,0:T(8,128)S(1)}, u32[]{:S(2)}) copy-start(f32[512,768]{1,0:T(8,128)S(1)} %get-tuple-element.89) | copy-start | bytes 4718596
  212.6 5.9 %slice-start.1 = ((s8[14155776]{0:T(1024)(128)(4,1)}), s8[4194304]{0:T(1024)(128)(4,1)S(1)}, s32[]{:S(2)}) async-start(s8[14155776]{0:T(1024)(128)(4,1)} %bitcast.263), calls=%async_computation.11 | async-start | bytes 8388608
  212.9 5.6 slice-start.2
  212.9 5.6 slice-start.3
  212.9 5.6 copy-start.41
  218.6 6.9 %copy-start.73 = (f32[512,4,768]{2,0,1:T(8,128)}, f32[512,4,768]{2,0,1:T(8,128)S(1)}, u32[]{:S(2)}) copy-start(f32[512,4,768]{2,0,1:T(8,128)S(1)} %fusion.26) | copy-start | bytes 18874372
  225.4 3.0 copy-start.74
  234.2 3.7 copy-start.1
  236.7 3.4 copy-start.8
  240.1 175.0 %reduce-scatter.3.cloned.1.call-start = ((), (), s32[]{:S(2)}) async-start(), calls=%async_computation.4 | async-start | bytes 15925248 | tf_op jit(solution)/shard_map/reduce_scatter | solution.py:212
  249.0 3.4 copy-start.15
  250.6 2.3 copy-start.7
  252.8 4.3 copy-start.75
  254.7 2.5 copy-start.21
  254.7 7.0 %slice-start.8 = ((s8[6291456]{0:T(1024)(128)(4,1)}), s8[4194304]{0:T(1024)(128)(4,1)S(1)}, s32[]{:S(2)}) async-start(s8[6291456]{0:T(1024)(128)(4,1)} %bitcast.304), calls=%async_computation.18 | async-start | bytes 8388608
  257.2 4.6 copy-start.42
  257.2 4.6 slice-start.9
  286.1 3.9 copy-start.34
  303.5 3.5 slice-start.4
  303.5 4.5 slice-start.6
  303.7 3.3 copy-start.32
  304.7 3.6 copy-start.25
  304.7 3.7 slice-start.5
  304.7 3.9 slice-start.7
  315.2 2.4 copy-start.16
  315.2 141.2 %reduce-scatter.5.cloned.1.call-start = ((), (), s32[]{:S(2)}) async-start(), calls=%async_computation.5 | async-start | bytes 2211840 | tf_op jit(solution)/shard_map/reduce_scatter | solution.py:213
  319.2 2.8 copy-start.47
  321.9 93.4 %copy-start.59 = (f32[4,768]{1,0:T(4,128)S(1)}, f32[4,768]{1,0:T(4,128)}, u32[]{:S(2)}) copy-start(f32[4,768]{1,0:T(4,128)} %get-tuple-element.98) | copy-start | bytes 36868
  415.1 151.2 %all-reduce.5.cloned.1.call-start = ((), (), s32[]{:S(2)}) async-start(), calls=%async_computation.3 | async-start | bytes 884736 | tf_op jit(solution)/shard_map/psum | solution.py:229
  415.9 6.3 %copy-start.55 = (f32[1,768]{1,0:T(1,128)S(1)}, f32[1,768]{1,0:T(1,128)}, u32[]{:S(2)}) copy-start(f32[1,768]{1,0:T(1,128)} %stack.93) | copy-start | bytes 9220
  415.9 6.3 %copy-start.56 = (f32[1,768]{1,0:T(1,128)S(1)}, f32[1,768]{1,0:T(1,128)}, u32[]{:S(2)}) copy-start(f32[1,768]{1,0:T(1,128)} %stack.94) | copy-start | bytes 9220
  415.9 6.3 %copy-start.57 = (f32[1,768]{1,0:T(1,128)S(1)}, f32[1,768]{1,0:T(1,128)}, u32[]{:S(2)}) copy-start(f32[1,768]{1,0:T(1,128)} %stack.92) | copy-start | bytes 9220
  415.9 6.3 %copy-start.58 = (f32[1,768]{1,0:T(1,128)S(1)}, f32[1,768]{1,0:T(1,128)}, u32[]{:S(2)}) copy-start(f32[1,768]{1,0:T(1,128)} %stack.95) | copy-start | bytes 9220
  422.2 34.3 %copy-start.71 = (bf16[768]{0:T(1024)(128)(2,1)S(1)}, bf16[768]{0:T(1024)(128)(2,1)}, u32[]{:S(2)}) copy-start(bf16[768]{0:T(1024)(128)(2,1)} %param.31) | copy-start | bytes 4612
  422.2 34.3 %copy-start.54 = (f32[4,768]{1,0:T(4,128)S(1)}, f32[4,768]{1,0:T(4,128)}, u32[]{:S(2)}) copy-start(f32[4,768]{1,0:T(4,128)} %copy-done.53) | copy-start | bytes 36868
  423.1 149.3 %all-gather.10.cloned.1.call-start = ((), (), s32[]{:S(2)}) async-start(), calls=%async_computation.6 | async-start | bytes 3981312 | tf_op jit(solution)/shard_map/all_gather | solution.py:214
  456.5 9.6 %copy-start.39 = (f32[512,768,1]{1,0,2:T(8,128)S(1)}, f32[512,768,1]{1,0,2:T(8,128)}, u32[]{:S(2)}) copy-start(f32[512,768,1]{1,0,2:T(8,128)} %get-tuple-element.93) | copy-start | bytes 4718596
  574.2 2.7 copy-start.4
  (30 other events, 41.6 us)
Sparse Core Ops, SparseCore 0:
  14.8 42.1 all-reduce.6
  151.4 45.4 all-gather.11
  240.2 45.9 all-gather.13
  315.3 99.7 reduce-scatter.2
  417.2 39.1 reduce-scatter.4
  458.3 33.2 all-gather.9
Sparse Core Ops, SparseCore 1:
  19.0 105.5 all-gather.7
  423.2 143.1 all-reduce.4

commit v2 on v1

--- a/solution.py
+++ b/solution.py
@@ -1,7 +1,14 @@
+import functools
+from types import SimpleNamespace
+
 import jax
 import jax.numpy as jnp
 from jax import lax
+from jax.experimental import pallas as pl
+from jax.experimental.pallas import tpu as pltpu
 from jax.sharding import PartitionSpec as P
+
+MESH = pl.DeviceIdType.MESH
 
 HD = 64
 BLOCK = 64
@@ -52,12 +59,967 @@
     return ein("the,hde->thd", low, weight), ein("thd,the->hde", q, low), jnp.sum(du, axis=0)
 
 
-def merge_heads(gathered):
-    tp, rows, three, width = gathered.shape
-    return gathered.transpose(1, 2, 0, 3).reshape(rows, three, tp * width)
+HD = 64
+BLOCK = 64
+CHUNK = 256
+EPSILON = 1e-05
+F32 = jnp.float32
+BF16 = jnp.bfloat16
+ALL = ("dp", "ctx", "tp")
+
+
+def ein(spec, a, b):
+    return jnp.einsum(spec, a, b, preferred_element_type=F32)
+
+
+def layer_norm(v, gain, offset):
+    c = v - jnp.mean(v, axis=-1, keepdims=True)
+    r = lax.rsqrt(jnp.mean(c * c, axis=-1, keepdims=True) + EPSILON)
+    n = c * r
+    return n * gain + offset, n, r
+
+
+def layer_norm_back(e, n, r, gain):
+    m = e * gain
+    back = r * (
+        m - jnp.mean(m, axis=-1, keepdims=True) - n * jnp.mean(m * n, axis=-1, keepdims=True)
+    )
+    return back, jnp.sum(e * n, axis=0), jnp.sum(e, axis=0)
+
+
+def gelu_parts(s):
+    t = jnp.tanh(0.7978845608028654 * (s + 0.044715 * s * s * s))
+    slope = 0.7978845608028654 * (1.0 + 3.0 * 0.044715 * s * s)
+    return 0.5 * s * (1.0 + t), 0.5 * (1.0 + t) + 0.5 * s * (1.0 - t * t) * slope
+
+
+def feature_map(q, weight, offset):
+    u = ein("thd,hde->the", q, weight) + offset
+    up, down = jax.nn.softmax(u, axis=-1), jax.nn.softmax(-u, axis=-1)
+    return up, down, jnp.concatenate([up, down], axis=-1).astype(BF16)
+
+
+def feature_back(delta, up, down, q, weight):
+    d, dd = delta[..., :HD], delta[..., HD:]
+    du = up * (d - jnp.sum(up * d, axis=-1, keepdims=True)) - down * (
+        dd - jnp.sum(down * dd, axis=-1, keepdims=True)
+    )
+    low = du.astype(BF16)
+    return ein("the,hde->thd", low, weight), ein("thd,the->hde", q, low), jnp.sum(du, axis=0)
+
+
+def place():
+    d, c, t = lax.axis_index("dp"), lax.axis_index("ctx"), lax.axis_index("tp")
+    y, core = c // 2, lax.rem(c, 2)
+    return SimpleNamespace(d=d, c=c, t=t, y=y, core=core, q=d * 2 + y,
+        x_nb=(1 - d, c, t), y_nb=(d, (1 - y) * 2 + core, t), core_nb=(d, y * 2 + 1 - core, t),
+        qx=(1 - d) * 2 + y, qy=d * 2 + 1 - y, qd=(1 - d) * 2 + 1 - y)
+
+def greet(p):
+    bar = pltpu.get_barrier_semaphore()
+    peers = [p.x_nb, p.y_nb, p.core_nb] + [(p.d, p.c, lax.rem(p.t + k, 4)) for k in (1, 2, 3)]
+    for peer in peers:
+        pl.semaphore_signal(bar, inc=1, device_id=peer, device_id_type=MESH)
+    pl.semaphore_wait(bar, len(peers))
+
+def nearest(t):
+    return [
+        jnp.where(t < 2, 1, 3),
+        jnp.where(t == 0, 2, jnp.where(t == 1, 3, jnp.where(t == 2, 1, 2))),
+        jnp.where(t == 0, 3, jnp.where(t == 3, 1, 2)),
+    ]
+
+
+class Gather:
+    def __init__(self, p, buf, sems, index):
+        self.p, self.buf, self.sems, self.i = p, buf, sems, index
+        self.rows = buf.shape[1]
+        self.piece = self.rows // 8
+        self.half = self.piece // 2
+        self.sent = []
+    def at(self, t, q, core, half=None):
+        start = q * (2 * self.piece) + core * self.piece
+        size = self.piece
+        if half is not None:
+            start, size = start + half * self.half, self.half
+        return self.buf.at[t, pl.ds(pl.multiple_of(start, 16), size)]
+    def shard(self, k): return lax.rem(self.p.t + k, 4)
+    def copy(self, ref, kind, k, peer):
+        s = self.sems[kind]
+        return pltpu.make_async_remote_copy(ref, ref, s.at[0, self.i, k - 1], s.at[1, self.i, k - 1], device_id=peer, device_id_type=MESH)
+    def go(self, *a):
+        c = self.copy(*a); c.start(); self.sent.append(c)
+    def first(self):
+        p = self.p
+        for k in (1, 2, 3):
+            ref = self.at(p.t, p.q, p.core)
+            s = self.sems["z"]
+            c = pltpu.make_async_remote_copy(ref, ref, s.at[0, self.i, k - 1], s.at[1, self.i, 3 - k], device_id=(p.d, p.c, lax.rem(p.t + k, 4)), device_id_type=MESH)
+            c.start(); self.sent.append(c)
+    def z(self, k):
+        p, t = self.p, self.shard(k)
+        ref = self.at(t, p.q, p.core)
+        self.copy(ref, "z", k, p.x_nb).wait_recv()
+        self.go(ref, "x", k, p.x_nb); self.go(ref, "y", k, p.y_nb)
+    def hop(self, ref, ok, up, k_there):
+        p = self.p; s = self.sems["z"]
+        i = self.nz; self.nz += 1
+        c = pltpu.make_async_remote_copy(ref, ref, s.at[0, self.i, i], s.at[1, self.i, k_there - 1],
+            device_id=(p.d, p.c, jnp.where(up, p.t + 1, p.t - 1)), device_id_type=MESH)
+        @pl.when(ok)
+        def _(): c.start()
+        self.cond.append((ok, c))
+    def first_hop(self):
+        p = self.p; self.nz = 0; self.cond = []
+        ref = self.at(p.t, p.q, p.core)
+        self.hop(ref, p.t < 3, True, 3)
+        self.hop(ref, p.t > 0, False, 1)
+    def zf(self, k):
+        p, t = self.p, self.shard(k)
+        ref = self.at(t, p.q, p.core)
+        self.copy(ref, "z", k, p.x_nb).wait_recv()
+        up = t < p.t
+        self.hop(ref, jnp.where(up, p.t < 3, p.t > 0), up, jnp.where(up, k - 1, k + 1))
+        self.go(ref, "x", k, p.x_nb); self.go(ref, "y", k, p.y_nb)
+    def drain_hops(self):
+        for ok, c in self.cond:
+            @pl.when(ok)
+            def _(): c.wait_send()
+    def xy(self, k):
+        p, t = self.p, self.shard(k)
+        self.copy(self.at(t, p.qx, p.core), "x", k, p.x_nb).wait_recv()
+        self.go(self.at(t, p.qx, p.core, 0), "fy", k, p.y_nb)
+        self.copy(self.at(t, p.qy, p.core), "y", k, p.y_nb).wait_recv()
+        self.go(self.at(t, p.qy, p.core, 1), "fx", k, p.x_nb)
+    def diag(self, k):
+        p, t = self.p, self.shard(k)
+        self.copy(self.at(t, p.qd, p.core, 0), "fy", k, p.y_nb).wait_recv()
+        self.copy(self.at(t, p.qd, p.core, 1), "fx", k, p.x_nb).wait_recv()
+        for q in range(4):
+            self.go(self.at(t, q, p.core), "c", k, p.core_nb)
+    def done(self, k):
+        p, t = self.p, self.shard(k)
+        ref = self.buf.at[t, pl.ds(0, 4 * self.piece)]
+        s = self.sems["c"]
+        pltpu.make_async_remote_copy(ref, ref, s.at[0, self.i, k - 1], s.at[1, self.i, k - 1], device_id=p.core_nb, device_id_type=MESH).wait_recv()
+    def drain(self):
+        for c in self.sent:
+            c.wait_send()
+
+
+class Reduce:
+    def __init__(self, p, i, G, X1, Y1, X2, Y2, Z, F, OUT, sems, own):
+        self.p, self.i, self.G, self.OUT, self.sems = p, i, G, OUT, sems
+        self.X1, self.Y1, self.X2, self.Y2, self.Z = X1, Y1, X2, Y2, Z
+        self.half = G.shape[1]; self.qr = self.half // 4; self.hr = self.qr // 2
+        self.sent = []
+        self.F, self.own = F, own
+    def t(self, k): return lax.rem(self.p.t + k, 4)
+    def rows(self, q, h): return pl.ds(pl.multiple_of(q * self.qr + h * self.hr, 16), self.hr)
+    def rdma(self, src, dst, kind, k, peer, k_there=None):
+        s = self.sems[kind]
+        return pltpu.make_async_remote_copy(src, dst, s.at[0, self.i, k], s.at[1, self.i, k if k_there is None else k_there], device_id=peer, device_id_type=MESH)
+    def go(self, *a):
+        c = self.rdma(*a); c.start(); self.sent.append(c)
+    def got(self, ref, kind, k):
+        self.rdma(ref, ref, kind, k, self.p.x_nb).wait_recv()
+    def one(self, k):
+        p, t = self.p, self.t(k)
+        for j in range(2):
+            self.go(self.G.at[t, self.rows((1 - p.d) * 2 + j, 0)], self.X1.at[k, j], "x1", k, p.x_nb)
+            self.go(self.G.at[t, self.rows(j * 2 + 1 - p.y, 1)], self.Y1.at[k, j], "y1", k, p.y_nb)
+    def two(self, k):
+        p, t, G = self.p, self.t(k), self.G
+        self.got(self.X1.at[k], "x1", k)
+        for j in range(2):
+            r = self.rows(p.d * 2 + j, 0)
+            G[t, r] = G[t, r] + self.X1[k, j]
+        self.go(G.at[t, self.rows(p.qy, 0)], self.Y2.at[k], "y2", k, p.y_nb)
+        self.got(self.Y1.at[k], "y1", k)
+        for j in range(2):
+            r = self.rows(j * 2 + p.y, 1)
+            G[t, r] = G[t, r] + self.Y1[k, j]
+        self.go(G.at[t, self.rows(p.qx, 1)], self.X2.at[k], "x2", k, p.x_nb)
+    def three(self, k):
+        p, t, G = self.p, self.t(k), self.G
+        for h, (kind, R) in enumerate((("y2", self.Y2), ("x2", self.X2))):
+            self.got(R.at[k], kind, k)
+            r = self.rows(p.q, h)
+            G[t, r] = G[t, r] + R[k]
+        if not isinstance(k, int):
+            whole = pl.ds(pl.multiple_of(p.q * self.qr, 16), self.qr)
+            self.go(G.at[t, whole], self.Z.at[3 - k], "z", k - 1, (p.d, p.c, t), 3 - k)
+    def piece(self, q, core, h=None):
+        start, size = core * self.half + q * self.qr, self.qr
+        if h is not None: start, size = start + h * self.hr, self.hr
+        return self.OUT.at[pl.ds(pl.multiple_of(start, 16), size)]
+    def final(self):
+        p = self.p
+        whole = pl.ds(pl.multiple_of(p.q * self.qr, 16), self.qr)
+        total = self.G[p.t, whole].astype(F32)
+        for k in range(3):
+            self.got(self.Z.at[k], "z", k)
+            total = total + self.Z[k].astype(F32)
+        ref = self.piece(p.q, p.core)
+        self.F[...] = total.astype(BF16)
+        self.go(self.F, ref, "f", 0, p.x_nb)
+        self.go(self.F, ref, "f", 1, p.y_nb)
+        pltpu.make_async_copy(self.F, ref, self.own.at[self.i]).start()
+
+    def spread(self):
+        p = self.p
+        ref = self.piece(p.qx, p.core); self.got(ref, "f", 0)
+        ref = self.piece(p.qx, p.core, 0); self.go(ref, ref, "f", 2, p.y_nb)
+        ref = self.piece(p.qy, p.core); self.got(ref, "f", 1)
+        ref = self.piece(p.qy, p.core, 1); self.go(ref, ref, "f", 3, p.x_nb)
+    def corner(self):
+        p = self.p
+        pltpu.make_async_copy(self.F, self.piece(p.q, p.core), self.own.at[self.i]).wait()
+        self.got(self.piece(p.qd, p.core, 0), "f", 2); self.got(self.piece(p.qd, p.core, 1), "f", 3)
+        ref = self.OUT.at[pl.ds(pl.multiple_of(p.core * self.half, 16), self.half)]
+        self.go(ref, ref, "f", 4, p.core_nb)
+    def end(self):
+        p = self.p
+        ref = self.OUT.at[pl.ds(pl.multiple_of((1 - p.core) * self.half, 16), self.half)]
+        self.got(ref, "f", 4)
+        for c in self.sent: c.wait_send()
+
+
+GATHER_SEMS = ("z", "x", "y", "fx", "fy", "c")
+SEMS = ("x1", "y1", "x2", "y2", "z", "f")
+
+
+def dot(a, b, ca, cb):
+    return lax.dot_general(a, b, (((ca,), (cb,)), ((), ())), preferred_element_type=F32)
+
+
+def loop(n, step):
+    def body(i, carry):
+        step(i)
+        return carry
+
+    lax.fori_loop(0, n, body, 0)
+
+
+def ds(i, n):
+    return pl.ds(pl.multiple_of(i * n, n), n)
+
+
+class Scan:
+    GROUPS = 3
+
+    def __init__(self, p, later, total, pair, up, down, got, sems):
+        self.p, self.later, self.total, self.pair_ref, self.up_ref, self.down_ref = p, later, total, pair, up, down
+        self.from_core, self.from_y, self.from_below, self.from_above = [got.at[i] for i in range(4)]
+        self.sems = sems
+        self.sent = []
+
+    def rdma(self, src, dst, i, peer):
+        return pltpu.make_async_remote_copy(
+            src, dst, self.sems.at[0, i], self.sems.at[1, i], device_id=peer, device_id_type=MESH
+        )
+
+    def heads(self, g):
+        n = self.total.shape[0] // self.GROUPS
+        return pl.ds(g * n, n)
+
+    def begin(self):
+        t = self.p.t
+
+        @pl.when(t == 0)
+        def _():
+            self.from_below[...] = jnp.zeros_like(self.from_below)
+
+        @pl.when(t == 3)
+        def _():
+            self.from_above[...] = jnp.zeros_like(self.from_above)
+
+        c = self.rdma(self.total, self.from_core, 0, self.p.core_nb)
+        c.start()
+        self.sent.append(c)
+
+    def pair(self):
+        self.rdma(self.total, self.from_core, 0, self.p.core_nb).wait_recv()
+        self.pair_ref[...] = self.total[...] + self.from_core[...]
+        c = self.rdma(self.pair_ref, self.from_y, 1, self.p.y_nb)
+        c.start()
+        self.sent.append(c)
+
+    def column(self, g):
+        p, h = self.p, self.heads(g)
+        core, y = p.core.astype(F32), p.y.astype(F32)
+        if self.later:
+            core, y = 1.0 - core, 1.0 - y
+        return core * self.from_core[h].astype(F32) + y * self.from_y[h].astype(F32)
+
+    def wait_y(self):
+        self.rdma(self.pair_ref, self.from_y, 1, self.p.y_nb).wait_recv()
+
+    def hop(self, g, upward):
+        p, h, t = self.p, self.heads(g), self.p.t
+        got = self.from_below if upward else self.from_above
+        out = self.up_ref if upward else self.down_ref
+        peer = (p.d, p.c, t + 1 if upward else t - 1)
+        has, sends = (t > 0, t < 3) if upward else (t < 3, t > 0)
+        c = self.rdma(out.at[h], got.at[h], 2 + g + (0 if upward else self.GROUPS), peer)
+
+        @pl.when(has)
+        def _():
+            c.wait_recv()
+
+        @pl.when(sends)
+        def _():
+            value = self.column(g) + got[h].astype(F32)
+            if upward != self.later:
+                value = value + self.total[h].astype(F32)
+            out[h] = value.astype(BF16)
+            c.start()
+
+    def chain(self, first):
+        t = self.p.t
+
+        @pl.when(t < 2)
+        def _():
+            for g in range(self.GROUPS):
+                self.hop(g, first)
+
+        @pl.when(t >= 2)
+        def _():
+            for g in range(self.GROUPS):
+                self.hop(g, not first)
+
+    def sum(self, g):
+        h = self.heads(g)
+        return self.column(g) + self.from_below[h].astype(F32) + self.from_above[h].astype(F32)
+
+    def drain(self):
+        p, t = self.p, self.p.t
+        for c in self.sent:
+            c.wait_send()
+        for g in range(self.GROUPS):
+            h = self.heads(g)
+            for upward in (True, False):
+                out = self.up_ref if upward else self.down_ref
+                peer = (p.d, p.c, t + 1 if upward else t - 1)
+                c = self.rdma(out.at[h], out.at[h], 2 + g + (0 if upward else self.GROUPS), peer)
+
+                @pl.when(t < 3 if upward else t > 0)
+                def _(c=c):
+                    c.wait_send()
+
+
+def layer_rows(v):
+    c = v - jnp.mean(v, axis=-1, keepdims=True)
+    r = lax.rsqrt(jnp.mean(c * c, axis=-1, keepdims=True) + EPSILON)
+    return c * r, r
+
+
+def fold(v):
+    total = v[:8]
+    for i in range(1, v.shape[0] // 8):
+        total = total + v[8 * i : 8 * i + 8]
+    return total
+
+
+def layer_back(e, n, r, gain):
+    m = e * gain
+    return r * (
+        m - jnp.mean(m, axis=-1, keepdims=True) - n * jnp.mean(m * n, axis=-1, keepdims=True)
+    )
+
+
+def block_kernel(m):
+    p = place()
+    t0 = p.t
+    X, CT, S, WA, W1, W2 = m.X, m.CT, m.S, m.WA, m.W1, m.W2
+    VEC, H1, H2, X2, ACC_O, ACC_E = m.vec, m.H1, m.H2, m.X2, m.ACC_O, m.ACC_E
+    MIX, PH, VX, AT, PX, SL, OT, RD = m.MIX, m.PH, m.VX, m.AT, m.PX, m.SL, m.OT, m.RD
+    A, DF, DNE, DU, GS = m.A, m.DF, m.DNE, m.DU, m.GS
+    FW, BC, IB, SUMS = m.FW, m.BC, m.IB, m.SUMS
+    ld = m.ld
+    loads = [
+        pltpu.make_async_copy(m.small, S.at[t0], ld.at[0]),
+        pltpu.make_async_copy(m.wm, WA.at[t0, pl.ds(0, 576)], ld.at[1]),
+        pltpu.make_async_copy(m.wo, WA.at[t0, pl.ds(576, 192)], ld.at[2]),
+        pltpu.make_async_copy(m.w1, W1.at[t0], ld.at[3]),
+        pltpu.make_async_copy(m.w2, W2.at[t0], ld.at[4]),
+        pltpu.make_async_copy(m.x, X, ld.at[5]),
+        pltpu.make_async_copy(m.g, CT, ld.at[6]),
+    ]
+    for c in loads:
+        c.start()
+    greet(p)
+    gsems = m.gather_sems
+    gs, gw, g1, g2 = gathers = [Gather(p, b, gsems, i) for i, b in enumerate((S, WA, W1, W2))]
+    for n, (g, ws) in enumerate(zip(gathers, ([0], [1, 2], [3], [4]))):
+        for i in ws:
+            loads[i].wait()
+        g.first() if n == 0 else g.first_hop()
+    K = nearest(t0)
+    shard = gs.shard
+
+    loads[5].wait()
+    loads[6].wait()
+
+    def norm1(i):
+        r = ds(i, 128)
+        n, _ = layer_rows(X[r].astype(F32))
+        H1[r] = (n * VEC[0:1] + VEC[1:2]).astype(BF16)
+
+    loop(4, norm1)
+    ones_row = jnp.where(lax.broadcasted_iota(jnp.int32, (16, 512), 0) == 0, 1.0, 0.0).astype(BF16)
+
+    def init(h):
+        VX[h, 64:80] = ones_row
+        DNE[h, 64:80] = jnp.zeros((16, 512), BF16)
+
+    loop(12, init)
+    SUMS[...] = jnp.zeros_like(SUMS)
+
+    def small(t):
+        rows = S[t, 192:208].astype(F32)
+        BC[t] = rows.T
+        rows = S[t, 208:224].astype(F32)
+        for i in range(6):
+            IB[t, :, 128 * i : 128 * i + 128] = rows[i : i + 1]
+        for h in range(3):
+            w = S[t, 64 * h : 64 * h + 64].astype(F32)
+            FW[0, t * 3 + h] = w[:, :64].astype(BF16)
+            FW[1, t * 3 + h] = w[:, 64:].astype(BF16)
+
+    def mix(t):
+        value = dot(WA[t, 0:576], H1[...], 1, 1)
+        for j in range(3):
+            for h in range(3):
+                n = j * 3 + h
+                part = (value[64 * n : 64 * n + 64] + BC[t, 0:64, n : n + 1]).astype(BF16)
+                if j < 2:
+                    MIX[t, 64 * n : 64 * n + 64] = part
+                else:
+                    VX[t * 3 + h, 0:64] = part
+
+    def features(t):
+        for h in range(3):
+            for i in range(2):
+                u = dot(FW[i, t * 3 + h], MIX[t, 192 * i + 64 * h : 192 * i + 64 * h + 64], 0, 0)
+                u = u + BC[t, 64 * i : 64 * i + 64, 9 + h : 10 + h]
+                e = jnp.exp(u - jnp.max(u, axis=0, keepdims=True))
+                PH[i, t * 3 + h, 0:64] = (e / jnp.sum(e, axis=0, keepdims=True)).astype(BF16)
+                e = jnp.exp(jnp.min(u, axis=0, keepdims=True) - u)
+                PH[i, t * 3 + h, 64:128] = (e / jnp.sum(e, axis=0, keepdims=True)).astype(BF16)
+
+    def states(t):
+        def one(i):
+            h = t * 3 + i
+            s0 = dot(VX[h, :, 0:256], PH[1, h, :, 0:256], 1, 1)
+            s1 = dot(VX[h, :, 256:512], PH[1, h, :, 256:512], 1, 1)
+            SL[h] = s0
+            m.TOT[h] = (s0 + s1).astype(BF16)
+
+        loop(3, one)
+
+    small(t0)
+    mix(t0)
+    features(t0)
+    states(t0)
+    for k in K:
+        gs.z(k)
+        gw.zf(k)
+    for k in K:
+        gs.xy(k)
+        gw.xy(k)
+    for k in K:
+        g1.zf(k)
+    for k in K:
+        gs.diag(k)
+        gw.diag(k)
+    for k in K:
+        g1.xy(k)
+    for n, k in enumerate(K):
+        gs.done(k)
+        gw.done(k)
+        t = shard(k)
+        small(t)
+        mix(t)
+        g2.zf(k)
+        features(t)
+        g1.diag(k)
+        states(t)
+
+    scan = Scan(p, False, m.TOT, m.PAIR, m.UP, m.DOWN, m.got_f, m.scan_f)
+    scan.begin()
+    causal = lax.broadcasted_iota(jnp.int32, (256, 256), 0) <= lax.broadcasted_iota(
+        jnp.int32, (256, 256), 1
+    )
+
+    def scores(h):
+        for j in range(2):
+            c = slice(256 * j, 256 * j + 256)
+            a = dot(PH[1, h, :, c], PH[0, h, :, c], 0, 0)
+            AT[h, j] = jnp.where(causal, a, 0.0).astype(BF16)
+
+    loop(3, scores)
+    scan.pair()
+    loop(3, lambda h: scores(h + 3))
+    for k in K:
+        g2.xy(k)
+    scan.wait_y()
+    scan.chain(True)
+    loop(6, lambda h: scores(h + 6))
+    scan.chain(False)
+    for g in range(scan.GROUPS):
+        value = scan.sum(g)
+        h = scan.heads(g)
+        PX[h, 0] = value.astype(BF16)
+        PX[h, 1] = (value + SL[h]).astype(BF16)
+
+    def attend(h):
+        for j in range(2):
+            c = slice(256 * j, 256 * j + 256)
+            num = dot(PX[h, j], PH[0, h, :, c], 1, 0) + dot(VX[h, :, c], AT[h, j], 1, 0)
+            r = 1.0 / num[64:65]
+            RD[h, :, c] = r
+            OT[ds(h, 64), c] = (num[0:64] * r).astype(BF16)
+
+    loop(12, attend)
+    for k in K:
+        g2.diag(k)
+
+    def norm2(i):
+        r = ds(i, 256)
+        total = X[r].astype(F32) + VEC[2:3]
+        for t in range(4):
+            total = total + dot(OT[192 * t : 192 * t + 192, r], WA[t, 576:768], 0, 0)
+        X2[r] = total
+        n, _ = layer_rows(total)
+        H2[r] = (n * VEC[3:4] + VEC[4:5]).astype(BF16)
+        ACC_O[r] = total + VEC[5:6]
+        ACC_E[r] = jnp.zeros((256, 768), F32)
+
+    loop(2, norm2)
+
+    sems = m.reduce_sems
+    land = (0, 1, 0, 3)
+    R = [
+        Reduce(p, i, m.G[i], *m.land[land[i]][1:], m.Z[i], m.F[i], m.outs[i], sems, m.own)
+        for i in range(4)
+    ]
+    CORE, core_sems, STAGE = [m.land[j][0] for j in land], m.r_core, m.STAGE
+    outgoing = []
+
+    def hand(i, k, value, slot):
+        t = shard(k)
+        if len(outgoing) >= 2:
+            outgoing[-2].wait_send()
+        STAGE[slot] = value(1 - p.core).astype(BF16)
+        c = pltpu.make_async_remote_copy(
+            STAGE.at[slot],
+            CORE[i].at[t],
+            core_sems.at[0, i, k],
+            core_sems.at[1, i, k],
+            device_id=p.core_nb,
+            device_id_type=MESH,
+        )
+        c.start()
+        outgoing.append(c)
+        R[i].G[t] = value(p.core).astype(BF16)
+
+    def meet(i, k):
+        t = shard(k)
+        G, C = R[i].G, CORE[i]
+        pltpu.make_async_remote_copy(
+            C.at[t],
+            C.at[t],
+            core_sems.at[0, i, k],
+            core_sems.at[1, i, k],
+            device_id=p.core_nb,
+            device_id_type=MESH,
+        ).wait_recv()
+
+        def add(j):
+            r = ds(j, 64)
+            G[t, r] = G[t, r] + C[t, r]
+
+        loop(G.shape[1] // 64, add)
+        R[i].one(k)
+
+    def hidden(t):
+        def rows(i):
+            r = ds(i, 256)
+            f = dot(H2[r], W1[t], 1, 0) + IB[t]
+            th = jnp.tanh(0.7978845608028654 * (f + 0.044715 * f * f * f))
+            a = (0.5 * f * (1.0 + th)).astype(BF16)
+            A[r] = a
+            slope = 0.5 * (1.0 + th) + 0.5 * f * (1.0 - th * th) * (
+                0.7978845608028654 * (1.0 + 3.0 * 0.044715 * f * f)
+            )
+            df = (dot(CT[r], W2[t], 1, 1) * slope).astype(BF16)
+            DF[r] = df
+            m.DIB[t] += fold(df.astype(F32))
+            ACC_O[r] += dot(a, W2[t], 1, 0)
+            ACC_E[r] += dot(df, W1[t], 1, 1)
+
+        loop(2, rows)
+
+    def lanes(core):
+        return pl.ds(pl.multiple_of(core * 384, 128), 384)
+
+    m.DIB[...] = jnp.zeros_like(m.DIB)
+    order = [0] + K
+    for n, k in enumerate(order):
+        t = shard(k)
+        if n:
+            g1.done(k)
+            g2.done(k)
+        hidden(t)
+        hand(0, k, lambda core: dot(A[:, lanes(core)], CT[...], 0, 0), 0)
+        hand(1, k, lambda core: dot(H2[:, lanes(core)], DF[...], 0, 0), 1)
+        if n >= 1:
+            R[0].two(order[n - 1])
+        if n >= 2:
+            R[0].three(order[n - 2])
+        meet(0, k)
+        if n >= 1:
+            R[1].two(order[n - 1])
+        if n >= 2:
+            R[1].three(order[n - 2])
+        meet(1, k)
+    A[...] = ACC_O[...].astype(BF16)
+    res_copy = pltpu.make_async_copy(A, m.result, ld.at[7])
+    res_copy.start()
+
+    def back2(i):
+        r = ds(i, 128)
+        n, s = layer_rows(X2[r])
+        e = ACC_E[r]
+        g = CT[r].astype(F32)
+        dx = g + layer_back(e, n, s, VEC[3:4])
+        SUMS[3] += fold(e * n)
+        SUMS[4] += fold(e)
+        SUMS[2] += fold(dx)
+        SUMS[5] += fold(g)
+        X2[r] = dx
+        H2[r] = dx.astype(BF16)
+
+    loop(4, back2)
+    DX, GG = X2, H2
+
+    for t in range(4):
+        value = dot(WA[t, 576:768], GG[...], 1, 1).astype(BF16).astype(F32)
+        for i in range(3):
+            h = 3 * t + i
+            do = value[64 * i : 64 * i + 64]
+            r = RD[h]
+            o = OT[64 * h : 64 * h + 64].astype(F32)
+            DNE[h, 0:64] = (do * r).astype(BF16)
+            dden = -jnp.sum(do * o, axis=0, keepdims=True) * r
+            DNE[h, 64:80] = jnp.where(
+                lax.broadcasted_iota(jnp.int32, (16, 512), 0) == 0, dden, 0.0
+            ).astype(BF16)
+    scan.drain()
+
+    def states_back(h):
+        s0 = dot(DNE[h, :, 0:256], PH[0, h, :, 0:256], 1, 1)
+        s1 = dot(DNE[h, :, 256:512], PH[0, h, :, 256:512], 1, 1)
+        SL[h] = s1
+        m.TOT[h] = (s0 + s1).astype(BF16)
+
+    loop(12, states_back)
+    scan = Scan(p, True, m.TOT, m.PAIR, m.UP, m.DOWN, m.got_b, m.scan_b)
+    scan.begin()
+    for i in range(2):
+        R[i].two(order[3])
+        R[i].three(order[2])
+
+    def feature_back(i, h, delta):
+        delta = delta.astype(BF16).astype(F32)
+        up, down = PH[i, h, 0:64].astype(F32), PH[i, h, 64:128].astype(F32)
+        d, dd = delta[0:64], delta[64:128]
+        du = up * (d - jnp.sum(up * d, axis=0, keepdims=True)) - down * (
+            dd - jnp.sum(down * dd, axis=0, keepdims=True)
+        )
+        DU[h, 64 * i : 64 * i + 64] = du.astype(BF16)
+
+    def query_back(h):
+        parts = []
+        for j in range(2):
+            c = slice(256 * j, 256 * j + 256)
+            dne = DNE[h, :, c]
+            m.DV[ds(h, 64), c] = dot(DNE[h, 0:64, c], AT[h, j], 1, 1).astype(BF16)
+            da = dot(VX[h, :, c], dne, 0, 0)
+            da = jnp.where(causal, da, 0.0).astype(BF16)
+            AT[h, j] = da
+            parts.append(dot(PH[1, h, :, c], da, 1, 0) + dot(PX[h, j], dne, 0, 0))
+        feature_back(0, h, jnp.concatenate(parts, axis=1))
+
+    loop(3, query_back)
+    scan.pair()
+    loop(3, lambda h: query_back(h + 3))
+    for i in range(2):
+        R[i].three(order[3])
+    for i in range(2):
+        R[i].final()
+    scan.wait_y()
+    scan.chain(True)
+    loop(6, lambda h: query_back(h + 6))
+    for i in range(2):
+        R[i].spread()
+    scan.chain(False)
+    for g in range(scan.GROUPS):
+        value = scan.sum(g)
+        h = scan.heads(g)
+        PX[h, 1] = value.astype(BF16)
+        PX[h, 0] = (value + SL[h]).astype(BF16)
+    for i in range(2):
+        R[i].corner()
+
+    def key_back(t, i):
+        h = t * 3 + i
+        parts, values = [], []
+        for j in range(2):
+            c = slice(256 * j, 256 * j + 256)
+            q = PX[h, j]
+            parts.append(dot(PH[0, h, :, c], AT[h, j], 1, 1) + dot(q, VX[h, :, c], 0, 0))
+            values.append(dot(q[0:64], PH[1, h, :, c], 1, 0))
+        feature_back(1, h, jnp.concatenate(parts, axis=1))
+        dv = jnp.concatenate(values, axis=1) + m.DV[ds(h, 64)].astype(F32)
+        MIX[t, 384 + 64 * i : 448 + 64 * i] = dv.astype(BF16)
+
+    ones8 = jnp.ones((8, 512), BF16)
+    left = lax.broadcasted_iota(jnp.int32, (64, 128), 1) < 64
+
+    def mixed_back(t, i):
+        h = t * 3 + i
+        du = DU[h]
+        rows = [slice(192 * k + 64 * i, 192 * k + 64 * i + 64) for k in range(3)]
+        GS[t, 64 * i : 64 * i + 64] = jnp.where(
+            left, dot(MIX[t, rows[0]], du, 1, 1), dot(MIX[t, rows[1]], du, 1, 1)
+        )
+        GS[t, 201 + i : 202 + i] = dot(ones8, du, 1, 1)[0:1]
+        for k in range(2):
+            MIX[t, rows[k]] = dot(FW[k, h], du[64 * k : 64 * k + 64], 1, 0).astype(BF16)
+        for k in range(3):
+            GS[t, 192 + 3 * k + i : 193 + 3 * k + i, 0:64] = dot(ones8, MIX[t, rows[k]], 1, 1)[0:1]
+
+    GS[:, 192:256] = jnp.zeros((4, 64, 128), F32)
+
+    for i in range(2):
+        R[i].end()
+    for n, k in enumerate(order):
+        t = shard(k)
+        for i in range(3):
+            key_back(t, i)
+            mixed_back(t, i)
+        for c in outgoing[-2:] if n == 0 else outgoing[-1:]:
+            c.wait_send()
+        STAGE[0] = dot(MIX[t, 0:384], H1[...], 1, 0).astype(BF16)
+        STAGE[1, 0:192] = dot(MIX[t, 384:576], H1[...], 1, 0).astype(BF16)
+        STAGE[1, 192:384] = dot(OT[ds(t, 192)], GG[...], 1, 0).astype(BF16)
+        c = pltpu.make_async_remote_copy(
+            STAGE.at[1 - p.core],
+            CORE[2].at[t],
+            core_sems.at[0, 2, k],
+            core_sems.at[1, 2, k],
+            device_id=p.core_nb,
+            device_id_type=MESH,
+        )
+        c.start()
+        outgoing.append(c)
+        R[2].G[t] = STAGE[p.core]
+        if n >= 1:
+            R[2].two(order[n - 1])
+        if n >= 2:
+            R[2].three(order[n - 2])
+        meet(2, k)
+
+    def back1(i):
+        r = ds(i, 256)
+        e = dot(MIX[0, :, r], WA[0, 0:576], 0, 0)
+        for t in range(1, 4):
+            e = e + dot(MIX[t, :, r], WA[t, 0:576], 0, 0)
+        n, s = layer_rows(X[r].astype(F32))
+        SUMS[0] += fold(e * n)
+        SUMS[1] += fold(e)
+        ACC_E[r] = DX[r] + layer_back(e, n, s, VEC[0:1])
+
+    loop(2, back1)
+    tok_copy = pltpu.make_async_copy(ACC_E, m.tokens_gradient, ld.at[8])
+    tok_copy.start()
+    for k in range(6):
+        row = jnp.sum(SUMS[k], axis=0, keepdims=True)
+        for i in range(6):
+            for t in range(4):
+                GS[t, 216 + 6 * k + i : 217 + 6 * k + i] = row[:, 128 * i : 128 * i + 128]
+    for t in range(4):
+        row = jnp.sum(m.DIB[t], axis=0, keepdims=True)
+        for i in range(6):
+            GS[t, 208 + i : 209 + i] = row[:, 128 * i : 128 * i + 128]
+    m.GB[...] = GS[...].astype(BF16)
+    small_sent = []
+    for k in order:
+        t = shard(k)
+        c = pltpu.make_async_remote_copy(
+            m.GB.at[t, pl.ds(pl.multiple_of((1 - p.core) * 128, 128), 128)],
+            CORE[3].at[t],
+            core_sems.at[0, 3, k],
+            core_sems.at[1, 3, k],
+            device_id=p.core_nb,
+            device_id_type=MESH,
+        )
+        c.start()
+        small_sent.append(c)
+        R[3].G[t] = m.GB[t, pl.ds(pl.multiple_of(p.core * 128, 128), 128)]
+    for k in order:
+        meet(3, k)
+    R[2].two(order[3])
+    R[2].three(order[2])
+    for k in order:
+        R[3].two(k)
+    R[2].three(order[3])
+    for k in order:
+        R[3].three(k)
+    for step in ("final", "spread", "corner", "end"):
+        for i in (2, 3):
+            getattr(R[i], step)()
+    scan.drain()
+    for c in outgoing[-1:] + small_sent:
+        c.wait_send()
+    for n, g in enumerate(gathers):
+        g.drain()
+        if n:
+            g.drain_hops()
+    res_copy.wait()
+    tok_copy.wait()
+
+
+def landing(rows, lanes):
+    h = rows // 2
+    q, r = h // 4, h // 8
+    shapes = ((4, h), (4, 2, r), (4, 2, r), (4, r), (4, r))
+    return [pltpu.VMEM((*shape, lanes), BF16) for shape in shapes]
+
+
+def block_call(x, g, wm, wo, w1, w2, small, vec):
+    rows, width = x.shape
+    flat = pltpu.VMEM((rows, width), BF16)
+    wide = pltpu.VMEM((rows, width), F32)
+    weights = pltpu.VMEM((4, 768, 768), BF16)
+    state = pltpu.VMEM((12, 80, 128), BF16)
+    packs = ((768, 768), (768, 768), (768, 768), (256, 128))
+    dma = pltpu.SemaphoreType.DMA
+    scratch = dict(
+        X=flat,
+        CT=flat,
+        S=pltpu.VMEM((4, 256, 128), BF16),
+        WA=weights,
+        W1=weights,
+        W2=weights,
+        H1=flat,
+        H2=flat,
+        X2=wide,
+        ACC_O=wide,
+        ACC_E=wide,
+        MIX=pltpu.VMEM((4, 576, rows), BF16),
+        PH=pltpu.VMEM((2, 12, 128, rows), BF16),
+        VX=pltpu.VMEM((12, 80, rows), BF16),
+        AT=pltpu.VMEM((12, 2, 256, 256), BF16),
+        PX=pltpu.VMEM((12, 2, 80, 128), BF16),
+        SL=pltpu.VMEM((12, 80, 128), F32),
+        OT=pltpu.VMEM((768, rows), BF16),
+        RD=pltpu.VMEM((12, 1, rows), F32),
+        A=flat,
+        DF=flat,
+        DNE=pltpu.VMEM((12, 80, rows), BF16),
+        DU=pltpu.VMEM((12, 128, rows), BF16),
+        DV=pltpu.VMEM((768, rows), BF16),
+        GS=pltpu.VMEM((4, 256, 128), F32),
+        GB=pltpu.VMEM((4, 256, 128), BF16),
+        FW=pltpu.VMEM((2, 12, 64, 64), BF16),
+        BC=pltpu.VMEM((4, 128, 16), F32),
+        IB=pltpu.VMEM((4, 1, 768), F32),
+        SUMS=pltpu.VMEM((6, 8, 768), F32),
+        DIB=pltpu.VMEM((4, 8, 768), F32),
+        TOT=state,
+        PAIR=state,
+        UP=state,
+        DOWN=state,
+        got_f=pltpu.VMEM((4, 12, 80, 128), BF16),
+        got_b=pltpu.VMEM((4, 12, 80, 128), BF16),
+        STAGE=pltpu.VMEM((2, 384, 768), BF16),
+        G=[pltpu.VMEM((4, n // 2, lanes), BF16) for n, lanes in packs],
+        Z=[pltpu.VMEM((3, n // 8, lanes), BF16) for n, lanes in packs],
+        F=[pltpu.VMEM((n // 8, lanes), BF16) for n, lanes in packs],
+        land={i: landing(*packs[i]) for i in (0, 1, 3)},
+        ld=dma((9,)),
+        own=dma((4,)),
+        r_core=dma((2, 4, 4)),
+        gather_sems={k: dma((2, 4, 5)) for k in GATHER_SEMS},
+        reduce_sems={k: dma((2, 4, 5)) for k in SEMS},
+        scan_f=dma((2, 8)),
+        scan_b=dma((2, 8)),
+    )
+    leaves, tree = jax.tree.flatten(scratch, is_leaf=lambda v: not isinstance(v, (dict, list)))
+    results = [
+        jax.ShapeDtypeStruct((rows, width), BF16),
+        jax.ShapeDtypeStruct((rows, width), F32),
+        *[jax.ShapeDtypeStruct(pack, BF16) for pack in packs],
+    ]
+
+    def body(x, g, wm, wo, w1, w2, small, vec, result, tokens_gradient, *rest):
+        outs, refs = rest[:4], rest[4:]
+        block_kernel(
+            SimpleNamespace(
+                x=x,
+                g=g,
+                wm=wm,
+                wo=wo,
+                w1=w1,
+                w2=w2,
+                small=small,
+                vec=vec,
+                result=result,
+                tokens_gradient=tokens_gradient,
+                outs=outs,
+                **jax.tree.unflatten(tree, refs),
+            )
+        )
+
+    anywhere = pl.BlockSpec(memory_space=pl.ANY)
+    return pl.pallas_call(
+        body,
+        out_shape=results,
+        in_specs=[anywhere] * 7 + [pl.BlockSpec(memory_space=pltpu.VMEM)],
+        out_specs=[anywhere] * len(results),
+        scratch_shapes=leaves,
+        compiler_params=pltpu.CompilerParams(
+            collective_id=0, has_side_effects=True, vmem_limit_bytes=67043328
+        ),
+        name="block",
+    )(x, g, wm, wo, w1, w2, small, vec)
+
+
+def small_pack(feature_weight, mixer_bias, feature_bias, inner_bias):
+    rows = jnp.concatenate(
+        [
+            feature_weight.transpose(1, 2, 0, 3).reshape(192, 128),
+            jnp.pad(mixer_bias.reshape(9, HD), ((0, 0), (0, HD))),
+            feature_bias.transpose(1, 0, 2).reshape(3, 128),
+            jnp.zeros((4, 128), feature_weight.dtype),
+            inner_bias.reshape(6, 128),
+        ]
+    )
+    return jnp.pad(rows, ((0, 42), (0, 0)))
+
+
+def small_unpack(small):
+    weights = small[:192].reshape(3, HD, 2, HD).transpose(2, 0, 1, 3)
+    mixer_bias = small[192:201, :HD].reshape(3, 3 * HD)
+    feature_bias = small[201:204].reshape(3, 2, HD).transpose(1, 0, 2)
+    return weights, mixer_bias, feature_bias, small[208:214].reshape(768), small[216:252].reshape(6, 768)
 
 
 def shards(
+    fast,
     tokens,
     first_gain,
     first_bias,
@@ -85,6 +1047,42 @@
     mine = lax.axis_index("ctx") * n_tp + lax.axis_index("tp")
 
     mixer_t = mixer_weight.transpose(1, 2, 0).reshape(-1, width)
+    if fast:
+        vec = jnp.stack(
+            [first_gain, first_bias, output_bias, second_gain, second_bias, outer_bias]
+        )
+        result, tokens_gradient, d_outer, d_inner, mixed, small = block_call(
+            tokens,
+            cotangent,
+            mixer_t,
+            output_weight,
+            inner_weight,
+            outer_weight,
+            small_pack(feature_weight, mixer_bias, feature_bias, inner_bias),
+            jnp.pad(vec.astype(F32), ((0, 2), (0, 0))),
+        )
+        d_feature, d_mixer_bias, d_feature_bias, d_inner_bias, shared = small_unpack(
+            small.astype(F32)
+        )
+        mixed = mixed.astype(F32)
+        return (
+            result,
+            tokens_gradient,
+            shared[0],
+            shared[1],
+            mixed[:576].reshape(3, heads_here * HD, width).transpose(2, 0, 1),
+            d_mixer_bias,
+            d_feature,
+            d_feature_bias,
+            mixed[576:],
+            shared[2],
+            shared[3],
+            shared[4],
+            d_inner.astype(F32),
+            d_inner_bias,
+            d_outer.astype(F32),
+            shared[5],
+        )
     sizes = [w.shape[0] for w in (mixer_t, output_weight, inner_weight, outer_weight)]
     pack = jnp.concatenate([mixer_t, output_weight, inner_weight, outer_weight], axis=0)
     part = pack.shape[0] // n_plane
@@ -295,4 +1293,5 @@
         P("tp", None),
         P(),
     )
-    return jax.shard_map(shards, mesh=mesh, in_specs=in_specs, out_specs=out_specs, check_vma=False)
+    fast = (mesh.shape["dp"], mesh.shape["ctx"], mesh.shape["tp"]) == (2, 4, 4)
+    return jax.shard_map(functools.partial(shards, fast), mesh=mesh, in_specs=in_specs, out_specs=out_specs, check_vma=False)

time: 596 us -> 246 us (0.41); the launches traced: 587 us -> 245 us
  waiting for transfers between devices: 373 us -> 0 us
  Pallas kernels: 0 us -> 221 us
  matrix products: 94.2 us -> 0 us
  local copies, waits for them, and re-layouts: 76.2 us -> 18.8 us
  other arithmetic: 25.4 us -> 4.61 us
  between operations: 17.8 us -> 0.7 us
    pallas_call x0 -> x1, Pallas kernels: none -> 221 us  [block_call(): pl.pallas_call(body, out_shape=results, in_specs=[anywhere] * 7 + [pl.Blo...]
    reduce_scatter x2 -> x0, waiting for transfers between devices: 126 us -> none  [the longest x1 92.7 us: shards(): big = lax.psum_scatter(big, ('dp', 'ctx'), scatter_dimension=0, tiled=True)]
    all_gather x4 -> x0, waiting for transfers between devices: 109 us -> none  [the longest x1 64.3 us: shards(): full = lax.all_gather(piece, ALL, axis=0, tiled=True)]
    psum x1 -> x0, waiting for transfers between devices: 98.7 us -> none  [shards(): lax.psum(jnp.concatenate([per_tp.reshape(-1), shared.reshape(-1)]), ALL)]
    dot_general x30 -> x0, matrix products: 83.7 us -> none  [the longest x28 76.1 us: ein(): return jnp.einsum(spec, a, b, preferred_element_type=F32)]
    unnamed x9 -> x0, waiting for transfers between devices: 39.1 us -> none
    unnamed x178 -> x12, local copies, waits for them, and re-layouts: 17.9 us -> 3.39 us
    reshape x18 -> x7, local copies, waits for them, and re-layouts: 18.1 us -> 3.81 us  [the longest x2 0.85 us: small_unpack(): weights = small[:192].reshape(3, HD, 2, HD).transpose(2, 0, 1, 3)]
  transfers between devices with their start and end apart: 8 -> 0, of which waited for: 7 -> 0; matrix products, arithmetic and copies ran while one was open for 14% -> 0% of each run, Pallas kernels for 0% -> 0%
where the time goes in v2:
time: 246 us; the launch traced here: 245 us
  Pallas kernels  221 us (90%)
  local copies, waits for them, and re-layouts  18.8 us (8%)
  other arithmetic  4.61 us (2%)
    pallas_call x1, Pallas kernels, block_call(): pl.pallas_call(body, out_shape=results, in_specs=[anywhere] * 7 + [pl.Blo...  221 us

profile of v2, /device:TPU:0, one launch (start us, length us, event | category | flops | bytes accessed | tf_op | source)
XLA Modules:
  0.0 245.5 jit_solution(8258405791098529587)
XLA Ops:
  0.6 0.8 reshape.78
  1.4 0.7 stack.21
  2.1 0.7 stack.22
  2.8 0.7 stack.23
  3.5 0.7 stack.24
  4.2 0.7 stack.25
  4.8 0.7 stack.26
  5.6 0.8 reshape.77
  6.3 0.6 pad_convert_fusion.vec
  7.0 1.0 copy.32
  7.9 0.1 reshape.76
  8.1 0.7 concatenate.3
  8.8 0.6 pad.15.small
  9.5 221.4 %block.1 = (bf16[512,768]{1,0:T(8,128)(2,1)}, f32[512,768]{1,0:T(8,128)}, bf16[768,768]{1,0:T(8,128)(2,1)}, bf16[768,768]{1,0:T(8,128)(2,1)}, bf16[768,768]{1,0:T(8,128)(2,1)}, /*index=5*/bf16[256,128]{1,0:T(8,128)(2,1)}) custom-call(bf16[512,768]{1,0:T(8,128)(2,1)} %x.7, bf16[512,768]{1,0:T(8,128)(2,1)} %g.1, bf16[576,768]{1,0:T(8,128)(2,1)} %bitcast.28, ...), custom_call_target="tpu_custom_call" | custom-call | tf_op jit(solution)/shard_map/block/pallas_call | solution.py:988
  230.8 0.0 copy-start
  230.8 0.8 slice.66
  231.6 0.7 reshape.83
  232.3 0.7 slice.64
  232.9 0.7 reshape.81
  233.6 0.8 slice.65
  234.4 0.8 convert_element_type.19
  235.3 0.6 slice_bitcast_fusion
  235.9 0.2 reshape.82
  236.1 0.7 copy.35
  236.8 0.0 copy-done
  236.8 0.9 slice.67
  237.6 0.0 copy-start.3
  237.6 1.3 slice.63
  238.9 0.5 copy-done.3
  239.4 0.0 copy-start.2
  239.4 1.6 convert_element_type.21
  241.0 0.1 copy-done.2
  241.1 0.0 copy-start.4
  241.1 1.6 convert_element_type.22
  242.7 0.0 copy-done.4
  242.7 0.0 copy-start.1
  242.7 0.9 copy.38
  243.5 0.8 copy-done.1
  244.3 1.1 copy.39
  (3 shorter events, 0.1 us)
Async XLA Ops:
  230.8 5.9 %copy-start = (bf16[768,768]{1,0:T(8,128)(2,1)S(1)}, bf16[768,768]{1,0:T(8,128)(2,1)}, u32[]{:S(2)}) copy-start(bf16[768,768]{1,0:T(8,128)(2,1)} %get-tuple-element.25) | copy-start | bytes 3538948
  237.6 1.8 copy-start.3
  239.4 1.7 copy-start.2
  241.1 1.6 copy-start.4
  242.7 1.7 copy-start.1
